TPU v7x, 512 devices: a whole 4x4x16 slice. The times are simulated.
512 devices in a mesh: ctx: 16 (over z), head: 8 (over y, core), seq: 4 (over x).
Axes of the slice: x: 4, y: 4, z: 16, core: 2. Of those that a mesh axis runs over, the one named last changes fastest.
Arguments:
- x_heads: bfloat16 [4, 64, 4096, 128], P('seq', 'head', 'ctx'), may hold values from -6 to 6
- target: bfloat16 [4, 64, 4096, 128], P('seq', 'head', 'ctx'), may hold values from -6 to 6
- b_proj: bfloat16 [4, 4096, 128], P('seq', 'ctx'), may hold values from -6 to 6
- c_proj: bfloat16 [4, 4096, 128], P('seq', 'ctx'), may hold values from -0.5 to 0.5
- dt_raw: float32 [4, 64, 4096], P('seq', 'head', 'ctx'), may hold values from -1.2 to 1.2
- a_log: float32 [64], P('head'), as said below
- skip_gain: float32 [64], P('head'), may hold values from 0.5 to 1.5
- dt_bias: float32 [64], P('head'), may hold values from -4.5 to -3.5
Outputs:
- grad_x: bfloat16 [4, 64, 4096, 128], P('seq', 'head', 'ctx')
- grad_b: float32 [4, 4096, 128], P('seq', ('ctx', 'head'))
- grad_c: float32 [4, 4096, 128], P('seq', ('ctx', 'head'))
- grad_dt_raw: float32 [4, 64, 4096], P('seq', 'head', 'ctx')
- grad_a_log: float32 [64], P('head')
- grad_skip: float32 [64], P('head')
- grad_dt_bias: float32 [64], P('head')
Inputs may be any that keep to these rules, and one draw needn't show every extreme that they name: exp(a_log) lies between 16 / 4096 and 3.
All inputs are finite; a program needn't handle non-finite values.
Results may differ from a plain program's by a relative error of at most 0.0054.
Values sent between devices are 32-bit elements; how exact they have to be, the bound alone decides.
A program may use at most 64 MiB of HBM per device.

v0:
```python
import jax
import jax.numpy as jnp
from jax import lax
from jax.sharding import PartitionSpec as P

GROUP = 256


highest = lax.Precision.HIGHEST


def carried_in(part, axis, combine, identity, reverse):
    count = lax.axis_size(axis)
    place = lax.axis_index(axis)
    ahead = count - 1 - place if reverse else place
    gathered = jax.tree.map(lambda a: lax.all_gather(a, axis), part)
    state = jax.tree.map(lambda a, e: jnp.zeros_like(a) + jnp.asarray(e, a.dtype), part, identity)

    def one(turn, state):
        source = count - 1 - turn if reverse else turn
        return combine(
            state, jax.tree.map(lambda a: lax.dynamic_index_in_dim(a, source, 0, False), gathered)
        )

    return lax.fori_loop(0, ahead, one, state)


def block_logs(dt_block, decay_rate):
    return jnp.cumsum(-decay_rate[:, None] * dt_block, axis=-1)


def state_part(x_block, b_block, dt_block, log_decay):
    weights = jnp.exp(log_decay[:, -1:] - log_decay) * dt_block
    scaled = (x_block.astype(jnp.float32) * weights[:, :, None]).astype(jnp.bfloat16)
    contrib = jnp.einsum("hjp,jn->hpn", scaled, b_block, preferred_element_type=jnp.float32)
    return (weights, scaled, contrib, jnp.exp(log_decay[:, -1]))


def intra_parts(b_block, c_block, dt_block, log_decay):
    block_size = log_decay.shape[-1]
    row_ids = lax.broadcasted_iota(jnp.int32, (block_size, block_size), 0)
    column_ids = lax.broadcasted_iota(jnp.int32, (block_size, block_size), 1)
    causal = (row_ids >= column_ids)[None]
    log_gaps = log_decay[:, :, None] - log_decay[:, None, :]
    decays = jnp.where(causal, jnp.exp(jnp.where(causal, log_gaps, 0.0)), 0.0)
    scores = jnp.einsum("in,jn->ij", c_block, b_block, preferred_element_type=jnp.float32)
    mixing = (scores[None] * decays * dt_block[:, None, :]).astype(jnp.bfloat16)
    return (decays, scores, mixing)


def forward_block(x_block, t_block, c_block, log_decay, skip_gain, start_state, mixing):
    inner = jnp.einsum("hij,hjp->hip", mixing, x_block, preferred_element_type=jnp.float32)
    state_low = start_state.astype(jnp.bfloat16)
    growth = jnp.exp(log_decay)[:, :, None]
    carried = (
        jnp.einsum("in,hpn->hip", c_block, state_low, preferred_element_type=jnp.float32) * growth
    )
    out_error = (
        inner
        + carried
        + skip_gain[:, None, None] * x_block.astype(jnp.float32)
        - t_block.astype(jnp.float32)
    )
    error_weighted = (out_error * growth).astype(jnp.bfloat16)
    pulled = jnp.einsum("hip,in->hpn", error_weighted, c_block, preferred_element_type=jnp.float32)
    return (out_error, carried, error_weighted, state_low, pulled)


def backward_local(
    x_block,
    b_block,
    c_block,
    dt_block,
    skip_gain,
    out_error,
    carried,
    error_weighted,
    state_low,
    decays,
    scores,
    mixing,
):
    error_low = out_error.astype(jnp.bfloat16)
    grad_mixing = jnp.einsum("hip,hjp->hij", error_low, x_block, preferred_element_type=jnp.float32)
    grad_in = (
        jnp.einsum("hij,hip->hjp", mixing, error_low, preferred_element_type=jnp.float32)
        + skip_gain[:, None, None] * out_error
    )
    masked = grad_mixing * decays
    grad_score = (masked * dt_block[:, None, :]).astype(jnp.bfloat16)
    grad_c = jnp.einsum("hij,jn->in", grad_score, b_block, preferred_element_type=jnp.float32)
    grad_c = grad_c + jnp.einsum(
        "hip,hpn->in", error_weighted, state_low, preferred_element_type=jnp.float32
    )
    grad_b = jnp.einsum("hij,in->jn", grad_score, c_block, preferred_element_type=jnp.float32)
    product = masked * scores[None]
    column_sum = jnp.sum(product, axis=1)
    row_sum = jnp.einsum("hij,hj->hi", product, dt_block, precision=highest)
    grad_logs = row_sum - column_sum * dt_block + jnp.sum(out_error * carried, axis=-1)
    grad_skip = jnp.sum(out_error * x_block.astype(jnp.float32), axis=(1, 2))
    return (grad_in, grad_c, grad_b, column_sum, grad_logs, grad_skip)


def backward_state(x_block, b_block, log_decay, weights, scaled, start_state, end_adjoint):
    adjoint_low = end_adjoint.astype(jnp.bfloat16)
    grad_b = jnp.einsum("hjp,hpn->jn", scaled, adjoint_low, preferred_element_type=jnp.float32)
    grad_scaled = jnp.einsum(
        "jn,hpn->hjp", b_block, adjoint_low, preferred_element_type=jnp.float32
    )
    grad_in = grad_scaled * weights[:, :, None]
    grad_weight = jnp.sum(grad_scaled * x_block.astype(jnp.float32), axis=-1)
    grad_step = grad_weight * jnp.exp(log_decay[:, -1:] - log_decay)
    grad_logs = -grad_weight * weights
    grad_final = jnp.sum(grad_weight * weights, axis=-1) + jnp.exp(log_decay[:, -1]) * jnp.sum(
        end_adjoint * start_state, axis=(1, 2)
    )
    return (grad_in, grad_b, grad_step, grad_logs, grad_final)


def finish_block(
    column_sum, grad_logs_a, grad_step_b, grad_logs_b, grad_final, dt_block, decay_rate
):
    grad_logs = grad_logs_a + grad_logs_b
    grad_logs = grad_logs.at[:, -1].add(grad_final)
    grad_log_rate = jnp.flip(jnp.cumsum(jnp.flip(grad_logs, axis=-1), axis=-1), axis=-1)
    grad_step = column_sum + grad_step_b - decay_rate[:, None] * grad_log_rate
    grad_alog = -decay_rate * jnp.sum(grad_log_rate * dt_block, axis=-1)
    return (grad_step, grad_alog)


def combine_maps(earlier, later):
    return (earlier[0] * later[0], later[0][:, None, None] * earlier[1] + later[1])


def on_device(x_heads, target, b_proj, c_proj, dt_raw, a_log, skip_gain, dt_bias):
    inputs_all = x_heads[0]
    target_all = target[0]
    b_rows = b_proj[0]
    c_rows = c_proj[0]
    decay_rate = jnp.exp(a_log)
    step_sizes = jax.nn.softplus(dt_raw[0] + dt_bias[:, None])
    head_count, positions, head_size = inputs_all.shape
    state_size = b_rows.shape[-1]
    block_count = positions // GROUP
    identity = (
        jnp.ones((head_count,), jnp.float32),
        jnp.zeros((head_count, head_size, state_size), jnp.float32),
    )
    summary = identity
    x_block = inputs_all
    t_block = target_all
    b_block = b_rows
    c_block = c_rows
    dt_block = step_sizes
    log_decay = block_logs(dt_block, decay_rate)
    weights, scaled, contrib, decay_total = state_part(x_block, b_block, dt_block, log_decay)
    pieces = [
        (
            x_block,
            t_block,
            b_block,
            c_block,
            dt_block,
            log_decay,
            weights,
            scaled,
            contrib,
            decay_total,
        )
    ]
    summary = combine_maps(summary, (decay_total, contrib))
    incoming = carried_in(summary, "ctx", combine_maps, identity, False)
    carry_state = incoming[1]
    block_index = 0
    (
        x_block,
        t_block,
        b_block,
        c_block,
        dt_block,
        log_decay,
        weights,
        scaled,
        contrib,
        decay_total,
    ) = pieces[block_index]
    decays, scores, mixing = intra_parts(b_block, c_block, dt_block, log_decay)
    out_error, carried, error_weighted, state_low, pulled = forward_block(
        x_block, t_block, c_block, log_decay, skip_gain, carry_state, mixing
    )
    local_parts = None
    forwards = [
        (
            carry_state,
            pulled,
            out_error,
            carried,
            error_weighted,
            state_low,
            decays,
            scores,
            mixing,
            local_parts,
        )
    ]
    adjoint_summary = identity
    for block_index in reversed(range(block_count)):
        adjoint_summary = combine_maps(
            adjoint_summary, (pieces[block_index][9], forwards[block_index][1])
        )
    adjoint_in = carried_in(adjoint_summary, "ctx", combine_maps, identity, True)
    end_adjoint = adjoint_in[1]
    grad_inputs = [None] * block_count
    grad_steps = [None] * block_count
    b_sums = [None] * block_count
    c_sums = [None] * block_count
    alog_sum = jnp.zeros((head_count,), jnp.float32)
    skip_sum = jnp.zeros((head_count,), jnp.float32)
    for block_index in reversed(range(block_count)):
        (
            x_block,
            t_block,
            b_block,
            c_block,
            dt_block,
            log_decay,
            weights,
            scaled,
            contrib,
            decay_total,
        ) = pieces[block_index]
        (
            start_state,
            pulled,
            out_error,
            carried,
            error_weighted,
            state_low,
            decays,
            scores,
            mixing,
            local_parts,
        ) = forwards[block_index]
        grad_in_b, grad_b_b, grad_step_b, grad_logs_b, grad_final = backward_state(
            x_block, b_block, log_decay, weights, scaled, start_state, end_adjoint
        )
        grad_in_a, grad_c_block, grad_b_a, column_sum, grad_logs_a, grad_skip_block = (
            backward_local(
                x_block,
                b_block,
                c_block,
                dt_block,
                skip_gain,
                out_error,
                carried,
                error_weighted,
                state_low,
                decays,
                scores,
                mixing,
            )
        )
        b_sums[block_index] = grad_b_a + grad_b_b
        c_sums[block_index] = grad_c_block
        grad_step, grad_alog = finish_block(
            column_sum, grad_logs_a, grad_step_b, grad_logs_b, grad_final, dt_block, decay_rate
        )
        grad_inputs[block_index] = (grad_in_a + grad_in_b).astype(jnp.bfloat16)
        grad_steps[block_index] = grad_step
        alog_sum = grad_alog
        skip_sum = grad_skip_block
        end_adjoint = decay_total[:, None, None] * end_adjoint + pulled
    grad_b, grad_c = (
        lax.psum_scatter(b_sums[0][None], "head", scatter_dimension=1, tiled=True),
        lax.psum_scatter(c_sums[0][None], "head", scatter_dimension=1, tiled=True),
    )
    grad_x = grad_inputs[0][None]
    grad_step_all = grad_steps[0]
    grad_raw = grad_step_all * jax.nn.sigmoid(dt_raw[0] + dt_bias[:, None])
    bias_sum = jnp.sum(grad_raw, axis=1)
    alog_all, skip_all, bias_all = lax.psum((alog_sum, skip_sum, bias_sum), ("ctx", "seq"))
    token_total = positions * lax.axis_size("ctx") * x_heads.shape[0] * lax.axis_size("seq")
    grad_a_log = alog_all / token_total
    grad_skip = skip_all / (token_total * head_size)
    grad_dt_bias = bias_all / token_total
    return (grad_x, grad_b, grad_c, grad_raw[None], grad_a_log, grad_skip, grad_dt_bias)


def solution(mesh):
    return jax.shard_map(
        on_device,
        mesh=mesh,
        in_specs=(
            P("seq", "head", "ctx", None),
            P("seq", "head", "ctx", None),
            P("seq", "ctx", None),
            P("seq", "ctx", None),
            P("seq", "head", "ctx"),
            P("head"),
            P("head"),
            P("head"),
        ),
        out_specs=(
            P("seq", "head", "ctx", None),
            P("seq", ("ctx", "head"), None),
            P("seq", ("ctx", "head"), None),
            P("seq", "head", "ctx"),
            P("head"),
            P("head"),
            P("head"),
        ),
        check_vma=False,
    )
```

profile of v0, /device:TPU:8, one launch (start us, length us, event | category | flops | bytes accessed | tf_op | source)
XLA Modules:
  0.0 428.4 jit_solution(2265389056122547225)
XLA Ops:
  7.3 1.3 fusion.48
  8.5 0.8 fusion.38
  9.3 0.6 reduce-window.14
  10.2 0.2 slice_reduce_fusion.2
  10.4 1.4 fusion.42
  11.8 2.5 convolution_add_fusion.3
  14.4 0.2 copy.62
  14.6 1.3 dynamic-slice.8
  16.5 0.2 dynamic-update-slice.3
  16.8 37.0 %all-reduce = f32[128]{0:T(128)S(1)} all-reduce(f32[128]{0:T(128)S(1)} %dynamic-update-slice.3), channel_id=2, replica_groups=mesh['ctx'=16,'head'=8,'seq'=4] {'ctx'}, use_global_device_ids=true, to_apply=%add | all-reduce | flops 128 | bytes 1024
  53.9 0.2 copy.64
  54.1 0.7 iota_compare_fusion
  54.8 0.2 fusion.34
  55.0 70.1 %all-gather.6.cloned.1.call-done = f32[128,128,128]{2,1,0:T(8,128)} async-done(((f32[8,128,128]{2,1,0:T(8,128)}), f32[128,128,128]{2,1,0:T(8,128)}) %all-gather.6.cloned.1.call-update) | async-done | bytes 8388624 | tf_op jit(solution)/shard_map/all_gather | solution.py:16
  125.1 0.3 fusion.6
  125.4 0.3 copy-done.10
  125.7 2.0 fusion.5
  127.8 1.1 convolution_add_fusion.2
  129.0 0.3 convolution_bitcast_fusion.1
  129.3 2.4 multiply_reduce_fusion
  131.8 0.8 fusion.9
  132.7 3.5 fusion.1
  136.2 109.0 %all-gather.8.cloned.1.call-done = f32[128,128,128]{2,1,0:T(8,128)} async-done(((f32[8,128,128]{2,1,0:T(8,128)}), f32[128,128,128]{2,1,0:T(8,128)}) %all-gather.8.cloned.1.call-update) | async-done | bytes 8388624 | tf_op jit(solution)/shard_map/all_gather | solution.py:16
  245.2 28.6 %while.28 = (s32[]{:T(128)}, f32[8,128,128]{2,1,0:T(8,128)S(1)}, s32[]{:T(128)}, f32[16,8]{1,0:T(8,128)}, f32[16,8,128,128]{3,2,1,0:T(8,128)}, /*index=5*/s32[]{:T(128)}, s32[]{:T(128)}, s32[]{:T(128)}, s32[]{:T(128)}) while((s32[]{:T(128)}, f32[8,128,128]{2,1,0:T(8,128)S(1)}, s32[]{:T(128)}, f32[16,8]{1,0:T(8,128)}, ...), condition=%wide.region_5.6_spmd, body=%wide.region_4.5_spmd.sunk | while | flops 262150 | bytes 1573115 | solution.py:25
  245.2 0.7 dynamic-slice_bitcast_fusion.5
  245.9 1.2 bitcast_add_fusion.7
  247.1 0.7 dynamic-slice_bitcast_fusion.5
  247.8 1.2 bitcast_add_fusion.7
  249.0 0.7 dynamic-slice_bitcast_fusion.5
  249.7 1.2 bitcast_add_fusion.7
  250.9 0.7 dynamic-slice_bitcast_fusion.5
  251.6 1.2 bitcast_add_fusion.7
  252.8 0.7 dynamic-slice_bitcast_fusion.5
  253.5 1.2 bitcast_add_fusion.7
  254.8 0.7 dynamic-slice_bitcast_fusion.5
  255.4 1.2 bitcast_add_fusion.7
  256.7 0.7 dynamic-slice_bitcast_fusion.5
  257.4 1.2 bitcast_add_fusion.7
  258.6 0.7 dynamic-slice_bitcast_fusion.5
  259.3 1.2 bitcast_add_fusion.7
  260.5 0.7 dynamic-slice_bitcast_fusion.5
  261.2 1.2 bitcast_add_fusion.7
  262.4 0.7 dynamic-slice_bitcast_fusion.5
  263.1 1.2 bitcast_add_fusion.7
  264.3 0.7 dynamic-slice_bitcast_fusion.5
  265.0 1.2 bitcast_add_fusion.7
  266.2 0.7 dynamic-slice_bitcast_fusion.5
  266.9 1.2 bitcast_add_fusion.7
  268.1 0.7 dynamic-slice_bitcast_fusion.5
  268.8 1.2 bitcast_add_fusion.7
  270.0 0.7 dynamic-slice_bitcast_fusion.5
  270.7 1.2 bitcast_add_fusion.7
  271.9 0.7 dynamic-slice_bitcast_fusion.5
  272.6 1.2 bitcast_add_fusion.7
  273.8 1.6 fusion.13
  275.4 0.3 convolution_bitcast_fusion.2
  276.1 0.9 fusion.8
  277.6 0.6 reduce-window.16
  278.6 0.8 fusion.46
  279.4 0.9 fusion.10
  280.4 139.4 %all-reduce.1 = (f32[8]{0:T(128)S(1)}, f32[8]{0:T(128)S(1)}, f32[8]{0:T(128)S(1)}) all-reduce(f32[8]{0:T(128)S(1)} %negate_multiply_fusion, f32[8]{0:T(128)S(1)} %get-tuple-element.179, f32[8]{0:T(128)S(1)} %get-tuple-element.207), channel_id=1, replica_groups=mesh['ctx'=16,'head'=8,'seq'=4] {'ctx','seq'}, use_global_device_ids=true, to_apply=%region_17.18 | all-reduce | flops 24 | bytes 192 | tf_op jit(solution)/shard_map/psum | solution.py:281
  419.8 0.5 broadcast_multiply_fusion.2
  420.3 1.0 copy.74
  421.3 0.5 broadcast_multiply_fusion
  (70 shorter events, 2.1 us)
Async XLA Ops:
  7.2 4.6 %copy-start = (bf16[1,256,128]{2,1,0:T(8,128)(2,1)S(1)}, bf16[1,256,128]{2,1,0:T(8,128)(2,1)}, u32[]{:S(2)}) copy-start(bf16[1,256,128]{2,1,0:T(8,128)(2,1)} %param.16) | copy-start | bytes 196612
  7.2 7.2 %copy-start.2 = (bf16[1,8,256,128]{3,2,1,0:T(8,128)(2,1)S(1)}, bf16[1,8,256,128]{3,2,1,0:T(8,128)(2,1)}, u32[]{:S(2)}) copy-start(bf16[1,8,256,128]{3,2,1,0:T(8,128)(2,1)} %param.14) | copy-start | bytes 1572868
  7.2 46.7 %copy-start.4 = (bf16[1,8,256,128]{3,2,1,0:T(8,128)(2,1)S(1)}, bf16[1,8,256,128]{3,2,1,0:T(8,128)(2,1)}, u32[]{:S(2)}) copy-start(bf16[1,8,256,128]{3,2,1,0:T(8,128)(2,1)} %param.15) | copy-start | bytes 1572868
  7.2 47.6 %copy-start.3 = (bf16[1,256,128]{2,1,0:T(8,128)(2,1)S(1)}, bf16[1,256,128]{2,1,0:T(8,128)(2,1)}, u32[]{:S(2)}) copy-start(bf16[1,256,128]{2,1,0:T(8,128)(2,1)} %param.17) | copy-start | bytes 196612
  7.2 117.8 %all-gather.6.cloned.1.call-start = ((), (), s32[]{:S(2)}) async-start(), calls=%async_computation.4 | async-start | bytes 8912896 | tf_op jit(solution)/shard_map/all_gather | solution.py:16
  10.2 4.2 copy-start.6
  10.4 4.0 copy-start.12
  11.8 2.6 copy-start.14
  14.3 230.9 %all-gather.8.cloned.1.call-start = ((), (), s32[]{:S(2)}) async-start(), calls=%async_computation.5 | async-start | bytes 8912896 | tf_op jit(solution)/shard_map/all_gather | solution.py:16
  125.1 0.6 copy-start.10
  125.7 2.0 copy-start.1
  125.7 2.0 copy-start.15
  127.8 1.6 copy-start.5
  127.8 1.6 copy-start.7
  127.8 1.5 copy-start.9
  128.9 292.9 %reduce-scatter.5.cloned.1.call-start = ((), (), s32[]{:S(2)}) async-start(), calls=%async_computation.3 | async-start | bytes 147456 | tf_op jit(solution)/shard_map/reduce_scatter | solution.py:275
  132.6 289.2 %reduce-scatter.3.cloned.1.call-start = ((), (), s32[]{:S(2)}) async-start(), calls=%async_computation.2 | async-start | bytes 147456 | tf_op jit(solution)/shard_map/reduce_scatter | solution.py:274
  275.4 0.7 copy-start.17
  276.1 2.5 copy-start.8
  276.1 2.5 copy-start.11
  276.1 2.5 copy-start.13
  276.1 2.5 copy-start.16
  276.1 4.2 copy-start.18
Sparse Core Ops, SparseCore 0:
  14.4 110.6 all-gather.5
  129.0 116.0 all-gather.7
  248.5 33.5 reduce-scatter.4
  285.4 37.3 reduce-scatter.2
where the time goes:
time: 430 us; the launch traced here: 428 us
  waiting for transfers between devices  179 us (42%)
  blocking collectives  176 us (41%)
  other arithmetic  25.5 us (6%)
  matrix products  16.9 us (4%)
  local copies, waits for them, and re-layouts  15.1 us (4%)
  between operations  14.7 us (3%)
    all_gather x2, waiting for transfers between devices, carried_in(): gathered = jax.tree.map(lambda a: lax.all_gather(a, axis), part)  179 us
    psum x1, blocking collectives, on_device(): lax.psum((alog_sum, skip_sum, bias_sum), ('ctx', 'seq'))  139 us
    unnamed x1, blocking collectives  37 us
    add x15, other arithmetic, combine_maps(): later[0][:, None, None] * earlier[1] + later[1]  17.8 us
    mul x15, local copies, waits for them, and re-layouts, combine_maps(): later[0][:, None, None] * earlier[1] + later[1]  10.4 us
  transfers between devices with their start and end apart: 4, of which 2 were waited for; matrix products, arithmetic and copies ran while one was open for 11% of the time, Pallas kernels for 0%

commit v1 on v0

v1 whole, which is shorter than its diff:
```python
import functools
import math

import jax
import jax.numpy as jnp
from jax import lax
from jax.experimental import pallas as pl
from jax.experimental.pallas import tpu as pltpu
from jax.sharding import PartitionSpec as P

LOG2E = math.log2(math.e)
PARTS = 2
HOP = (3, 2)
F32 = jnp.float32
BF16 = jnp.bfloat16
HIGHEST = lax.Precision.HIGHEST


def nn(a, b, precision=None):
    return lax.dot_general(a, b, (((1,), (0,)), ((), ())), precision=precision, preferred_element_type=F32)


def nt(a, b):
    return lax.dot_general(a, b, (((1,), (1,)), ((), ())), preferred_element_type=F32)


def tn(a, b):
    return lax.dot_general(a, b, (((0,), (0,)), ((), ())), preferred_element_type=F32)


def iota(shape, dim):
    return lax.broadcasted_iota(jnp.int32, shape, dim)


def column(ref, heads):
    eye = iota((heads, heads), 0) == iota((heads, heads), 1)
    spread = jnp.broadcast_to(ref[...], (heads, heads))
    return jnp.sum(jnp.where(eye, spread, 0.0), axis=1, keepdims=True)


def row_sums(values):
    high = values.astype(BF16)
    low = (values - high.astype(F32)).astype(BF16)
    both = jnp.concatenate([high, low], axis=1)
    return nt(jnp.ones((8, both.shape[1]), BF16), both)[0:1]


def kernel(
    sizes, x_ref, t_ref, b_ref, c_ref, dt_ref, alog_ref, skip_ref, bias_ref,
    gx_ref, gb_ref, gc_ref, gdt_ref, oalog_ref, oskip_ref, obias_ref,
    l_rows, r_rows, w_rows, g_rows, d_rows, lt_rows, s_rows, gl_rows, cq_rows, gf_rows, sk_rows,
    bt, ct, scores, cgt, decay, mixed, inner, g_cols, w_cols,
    contrib, srecv, snext, mbuf, wrecv, tbuf, pbuf, urecv,
    gst, gb_acc, gc_acc, rs_send, rs_recv, pz, px, pz_own, px_own,
    s_send, s_recv, w_send, w_recv, u_send, u_recv, rs_ss, rs_rs, pz_ss, pz_rs, px_ss, px_rs,
):
    nz, nh, ns = sizes
    heads, group, width = x_ref.shape[1:]
    state = b_ref.shape[2]
    piece = state // PARTS
    z = lax.axis_index("ctx")
    head_at = lax.axis_index("head")
    seq_at = lax.axis_index("seq")

    barrier = pltpu.get_barrier_semaphore()
    for name, at, count in (("ctx", z, nz), ("head", head_at, nh), ("seq", seq_at, ns)):
        for d in range(1, count):
            pl.semaphore_signal(
                barrier, inc=1, device_id={name: lax.rem(at + d, count)}, device_id_type=pl.DeviceIdType.MESH
            )

    rate = jnp.exp(column(alog_ref, heads))
    bias = column(bias_ref, heads)
    raw = dt_ref[0] + bias
    dt = jnp.maximum(raw, 0.0) + jnp.log1p(jnp.exp(-jnp.abs(raw)))
    upper = (iota((group, group), 0) <= iota((group, group), 1)).astype(F32)
    logs = nn(dt * (rate * -LOG2E), upper, HIGHEST)
    last = logs[:, group - 1 : group]
    rel = jnp.log(dt) * LOG2E - logs
    l_rows[...] = logs
    r_rows[...] = rel
    w_rows[...] = jnp.exp2(last + rel)
    g_rows[...] = jnp.exp2(logs)
    d_rows[...] = jnp.broadcast_to(jnp.exp2(last), (heads, width))
    lt_rows[...] = jnp.broadcast_to(last, (heads, width))
    s_rows[...] = jnp.broadcast_to(column(skip_ref, heads), (heads, width))
    bt[...] = b_ref[0].astype(F32).T
    ct[...] = c_ref[0].astype(F32).T
    scores[...] = nt(b_ref[0], c_ref[0])
    gst[...] = jnp.zeros_like(gst)
    gb_acc[...] = jnp.zeros_like(gb_acc)
    gc_acc[...] = jnp.zeros_like(gc_acc)

    pl.semaphore_wait(barrier, nz + nh + ns - 3)

    def chain(source, target, sends, receives, k, part, step):
        at = pl.ds(part * piece, piece)
        return pltpu.make_async_remote_copy(
            src_ref=source.at[k, at],
            dst_ref=target.at[k, at],
            send_sem=sends.at[k * PARTS + part],
            recv_sem=receives.at[k * PARTS + part],
            device_id={"ctx": lax.rem(z + step, nz)},
            device_id_type=pl.DeviceIdType.MESH,
        )

    def s_copy(k, part):
        return chain(snext, srecv, s_send, s_recv, k, part, 1)

    def w_copy(k, part):
        return chain(mbuf, wrecv, w_send, w_recv, k, part, nz - 1)

    def u_copy(k, part):
        return chain(pbuf, urecv, u_send, u_recv, k, part, nz - 1)

    def prepare(k):
        row = pl.ds(k, 1)
        contrib[k] = nn((bt[...] * w_rows[row, :]).astype(BF16), x_ref[0, k])
        scaled_c = (ct[...] * g_rows[row, :]).astype(BF16)
        cgt[...] = scaled_c
        mbuf[k] = nt(scaled_c, scaled_c)

    def pass_state(k):
        d = d_rows[pl.ds(k, 1), :]
        for part in range(PARTS):
            at = pl.ds(part * piece, piece)

            @pl.when(z > 0)
            def _():
                s_copy(k, part).wait_recv()
                snext[k, at] = d * srecv[k, at] + contrib[k, at]

            @pl.when(z == 0)
            def _():
                snext[k, at] = contrib[k, at]

            @pl.when(z < nz - 1)
            def _():
                s_copy(k, part).start()

        @pl.when(z == 0)
        def _():
            srecv[k] = jnp.zeros((state, width), F32)

    def pass_gram(k):
        d = d_rows[pl.ds(k, 1), :]
        for part in range(PARTS):
            at = pl.ds(part * piece, piece)

            @pl.when(z < nz - 1)
            def _():
                w_copy(k, part).wait_recv()
                mbuf[k, at] = (d * d) * wrecv[k, at] + mbuf[k, at]

            @pl.when(z > 0)
            def _():
                w_copy(k, part).start()

        @pl.when(z < nz - 1)
        def _():
            tbuf[k] = nn(wrecv[k], contrib[k], HIGHEST)

        @pl.when(z == nz - 1)
        def _():
            wrecv[k] = jnp.zeros((state, state), F32)
            urecv[k] = jnp.zeros((state, width), F32)

    def pass_adjoint(k):
        d = d_rows[pl.ds(k, 1), :]
        for part in range(PARTS):
            at = pl.ds(part * piece, piece)

            @pl.when(z < nz - 1)
            def _():
                u_copy(k, part).wait_recv()
                pbuf[k, at] = d * (urecv[k, at] + tbuf[k, at]) + pbuf[k, at]

            @pl.when(z > 0)
            def _():
                u_copy(k, part).start()

    def local(k):
        row = pl.ds(k, 1)
        logs_row = l_rows[row, :]
        rel_col = jnp.broadcast_to(r_rows[row, :], (width, group)).T
        logs_col = jnp.broadcast_to(logs_row, (width, group)).T
        g_cols[k] = jnp.exp2(logs_col)
        w_cols[k] = jnp.exp2(rel_col + lt_rows[row, :])
        gaps = jnp.concatenate([rel_col] * (group // width), axis=1) + logs_row
        causal = iota((group, group), 1) >= iota((group, group), 0)
        scaled_decay = jnp.exp2(jnp.where(causal, gaps, -1e30))
        decay[k] = scaled_decay
        mix = (scores[...] * scaled_decay).astype(BF16)
        mixed[k] = mix
        x = x_ref[0, k]
        within = tn(mix, x)
        inner[k] = within
        error = within + s_rows[row, :] * x.astype(F32) - t_ref[0, k].astype(F32)
        pbuf[k] = nn(cgt[...], error.astype(BF16))

    def finish(k):
        row = pl.ds(k, 1)
        skip = s_rows[row, :]
        x = x_ref[0, k]
        wide = x.astype(F32)
        state_low = srecv[k].astype(BF16)
        growth = g_cols[k]
        weights = w_cols[k]
        output = inner[k] + nn(c_ref[0], state_low) * growth
        error = output + skip * wide - t_ref[0, k].astype(F32)
        low = error.astype(BF16)
        gst[...] += nt(x, low) * decay[k]
        after = snext[k]
        adjoint = (urecv[k] + nn(wrecv[k], after, HIGHEST)).astype(BF16)
        grad = nn(mixed[k], low) + nn(b_ref[0], adjoint) * weights
        gx_ref[0, k] = (grad + skip * error).astype(BF16)
        gc_acc[...] += nt((error * growth).astype(BF16), state_low)
        gb_acc[...] += nt((wide * weights).astype(BF16), adjoint)
        pulled = wide * grad
        gl_rows[row, :] = row_sums(low.astype(F32) * output - pulled)
        cq_rows[row, :] = row_sums(pulled)
        gf_rows[row, :] = jnp.sum(adjoint.astype(F32) * after, axis=0, keepdims=True)
        sk_rows[row, :] = jnp.sum(error * wide, axis=0, keepdims=True)

    up, down = HOP
    s_at = (z * up) // down
    w_at = ((nz - 1 - z) * up) // down
    u_at = w_at + heads
    f_at = jnp.maximum(s_at, u_at)
    steps = ((nz - 1) * up) // down + 2 * heads

    def step(s, carry):
        def run(work, first):
            @pl.when(jnp.logical_and(s >= first, s < first + heads))
            def _():
                work(s - first)

        run(prepare, 0)
        run(pass_state, s_at)
        run(pass_gram, w_at)
        run(local, 0)
        run(pass_adjoint, u_at)
        run(finish, f_at)
        return carry

    lax.fori_loop(0, steps, step, 0)

    tokens = float(group * nz * ns)
    rising = nn(gl_rows[...], (iota((group, group), 0) >= iota((group, group), 1)).astype(F32), HIGHEST)
    rising = rising + jnp.sum(gf_rows[...], axis=1, keepdims=True)
    grad_raw = (cq_rows[...] / dt - rate * rising) * (1.0 / (1.0 + jnp.exp(-raw)))
    gdt_ref[0] = grad_raw
    totals = (
        jnp.sum(rising * dt, axis=1, keepdims=True) * (-rate / tokens),
        jnp.sum(sk_rows[...], axis=1, keepdims=True) / (tokens * width),
        jnp.sum(grad_raw, axis=1, keepdims=True) / tokens,
    )
    packed = jnp.zeros((heads, width), F32)
    for q, total in enumerate(totals):
        mine = iota((heads, width), 1) == iota((heads, width), 0) + q * heads
        packed = packed + jnp.where(mine, total, 0.0)
    pz_own[0] = jnp.sum(packed, axis=0, keepdims=True)

    def spread(name, at, count, source_of, target, sends, receives):
        copies = []
        for d in range(1, count):
            to = lax.rem(at + d, count)
            copies.append(
                pltpu.make_async_remote_copy(
                    src_ref=source_of(to),
                    dst_ref=target.at[d],
                    send_sem=sends.at[d],
                    recv_sem=receives.at[d],
                    device_id={name: to},
                    device_id_type=pl.DeviceIdType.MESH,
                )
            )
        for copy in copies:
            copy.start()
        return copies

    z_copies = spread("ctx", z, nz, lambda to: pz_own.at[0], pz, pz_ss, pz_rs)

    gs_low = gst[...].astype(BF16)
    grad_b = gb_acc[...] + nn(gs_low, c_ref[0])
    grad_c = gc_acc[...] + tn(gs_low, b_ref[0])
    rows = group // nh
    for r in range(nh):
        rs_send[r, 0:rows] = grad_b[r * rows : (r + 1) * rows]
        rs_send[r, rows : 2 * rows] = grad_c[r * rows : (r + 1) * rows]
    h_copies = spread("head", head_at, nh, lambda to: rs_send.at[to], rs_recv, rs_ss, rs_rs)

    total = pz_own[0]
    for d, copy in enumerate(z_copies, 1):
        copy.wait_recv()
        total = total + pz[d]
    px_own[0] = total
    x_copies = spread("seq", seq_at, ns, lambda to: px_own.at[0], px, px_ss, px_rs)

    whole = rs_send[head_at]
    for d, copy in enumerate(h_copies, 1):
        copy.wait_recv()
        whole = whole + rs_recv[d]
    gb_ref[0] = whole[0:rows]
    gc_ref[0] = whole[rows : 2 * rows]

    for d, copy in enumerate(x_copies, 1):
        copy.wait_recv()
        total = total + px[d]
    for q, out in enumerate((oalog_ref, oskip_ref, obias_ref)):
        turned = total if q == 0 else pltpu.roll(total, width - q * heads, 1)
        out[...] = turned[:, 0:heads]

    for copy in z_copies + h_copies + x_copies:
        copy.wait_send()

    def drain(k, carry):
        for part in range(PARTS):

            @pl.when(z < nz - 1)
            def _():
                s_copy(k, part).wait_send()

            @pl.when(z > 0)
            def _():
                w_copy(k, part).wait_send()
                u_copy(k, part).wait_send()

        return carry

    lax.fori_loop(0, heads, drain, 0)


def on_device(sizes, x, t, b, c, dt, a_log, skip, bias):
    nz, nh, ns = sizes
    _, heads, group, width = x.shape
    state = b.shape[2]
    rows = group // nh
    vmem = pl.BlockSpec(memory_space=pltpu.VMEM)
    whole = pltpu.VMEM((heads, state, width), F32)
    tall = pltpu.VMEM((heads, group, width), F32)
    line = pltpu.VMEM((heads, group), F32)
    short = pltpu.VMEM((heads, width), F32)
    flat = pltpu.VMEM((state, group), F32)
    square = pltpu.VMEM((group, group), F32)
    panel = pltpu.VMEM((group, width), F32)
    chain_sems = pltpu.SemaphoreType.DMA((heads * PARTS,))
    sems = [chain_sems] * 6
    for count in (nh, nz, ns):
        sems += [pltpu.SemaphoreType.DMA((count,))] * 2
    outs = pl.pallas_call(
        functools.partial(kernel, sizes),
        out_shape=(
            jax.ShapeDtypeStruct(x.shape, BF16),
            jax.ShapeDtypeStruct((1, rows, state), F32),
            jax.ShapeDtypeStruct((1, rows, state), F32),
            jax.ShapeDtypeStruct(dt.shape, F32),
        )
        + (jax.ShapeDtypeStruct((1, heads), F32),) * 3,
        in_specs=[vmem] * 8,
        out_specs=(vmem,) * 7,
        scratch_shapes=[line] * 4
        + [short] * 3
        + [line] * 2
        + [short] * 2
        + [
            flat,
            flat,
            square,
            pltpu.VMEM((state, group), BF16),
            pltpu.VMEM((heads, group, group), F32),
            pltpu.VMEM((heads, group, group), BF16),
            tall,
            tall,
            tall,
        ]
        + [whole] * 8
        + [
            square,
            panel,
            panel,
            pltpu.VMEM((nh, 2 * rows, width), F32),
            pltpu.VMEM((nh, 2 * rows, width), F32),
            pltpu.VMEM((nz, 1, width), F32),
            pltpu.VMEM((ns, 1, width), F32),
            pltpu.VMEM((1, 1, width), F32),
            pltpu.VMEM((1, 1, width), F32),
        ]
        + sems,
        compiler_params=pltpu.CompilerParams(collective_id=0, has_side_effects=True),
        name="mixer",
    )(x, t, b, c, dt, a_log.reshape(1, heads), skip.reshape(1, heads), bias.reshape(1, heads))
    return outs[:4] + tuple(o.reshape(heads) for o in outs[4:])


def solution(mesh):
    sizes = tuple(mesh.shape[name] for name in ("ctx", "head", "seq"))
    return jax.shard_map(
        functools.partial(on_device, sizes),
        mesh=mesh,
        in_specs=(
            P("seq", "head", "ctx", None),
            P("seq", "head", "ctx", None),
            P("seq", "ctx", None),
            P("seq", "ctx", None),
            P("seq", "head", "ctx"),
            P("head"),
            P("head"),
            P("head"),
        ),
        out_specs=(
            P("seq", "head", "ctx", None),
            P("seq", ("ctx", "head"), None),
            P("seq", ("ctx", "head"), None),
            P("seq", "head", "ctx"),
            P("head"),
            P("head"),
            P("head"),
        ),
        check_vma=False,
    )
```

time: 430 us -> 113 us (0.26)
  the two profiles are of different devices: /device:TPU:8 before, /device:TPU:1 now
where the time goes in v1:
time: 113 us
  Pallas kernels  107 us (95%)
  local copies, waits for them, and re-layouts  5.69 us (5%)
    pallas_call x1, Pallas kernels, on_device(): pl.pallas_call(functools.partial(kernel, sizes), out_shape=(jax.ShapeDtyp...  107 us
    unnamed x19, local copies, waits for them, and re-layouts  5.69 us

profile of v1, /device:TPU:1, one launch (start us, length us, event | category | flops | bytes accessed | tf_op | source)
XLA Modules:
  0.0 113.1 jit_solution(13957578848912330651)
XLA Ops:
  0.6 106.8 %mixer.1 = (bf16[1,8,256,128]{3,2,1,0:T(8,128)(2,1)}, f32[1,32,128]{2,1,0:T(8,128)}, f32[1,32,128]{2,1,0:T(8,128)}, f32[1,8,256]{2,1,0:T(8,128)}, f32[1,8]{1,0:T...) custom-call(bf16[1,8,256,128]{3,2,1,0:T(8,128)(2,1)} %x_ref.1, bf16[1,8,256,128]{3,2,1,0:T(8,128)(2,1)} %t_ref.1, ...), custom_call_target="tpu_custom_call" | custom-call | tf_op jit(solution)/shard_map/mixer/pallas_call | solution.py:351
  107.4 0.0 copy-start.1
  107.4 1.9 %copy.22 = bf16[1,8,256,128]{3,2,1,0:T(8,128)(2,1)} copy(bf16[1,8,256,128]{3,2,1,0:T(8,128)(2,1)} %get-tuple-element.28) | data formatting | bytes 1048576
  109.3 0.0 copy-done.1
  109.3 0.0 copy-start
  109.3 0.6 copy.23
  109.9 0.1 copy-done
  110.1 0.0 copy-start.2
  110.1 0.6 copy.24
  110.7 0.1 copy-done.2
  110.8 0.0 copy-start.5
  110.8 0.6 copy.25
  111.4 0.0 copy-done.5
  111.4 0.0 copy-start.4
  111.4 0.5 copy.26
  111.9 0.1 copy-done.4
  112.0 0.0 copy-start.3
  112.0 0.5 copy.27
  112.5 0.1 copy-done.3
  112.6 0.5 copy.28
Async XLA Ops:
  107.4 1.9 %copy-start.1 = (f32[1,32,128]{2,1,0:T(8,128)S(1)}, f32[1,32,128]{2,1,0:T(8,128)}, u32[]{:S(2)}) copy-start(f32[1,32,128]{2,1,0:T(8,128)} %get-tuple-element.29) | copy-start | bytes 49156
  109.3 0.7 copy-start
  110.1 0.7 copy-start.2
  110.8 0.6 copy-start.5
  111.4 0.6 copy-start.4
  112.0 0.6 copy-start.3

commit v2 on v1

v2 whole, which is shorter than its diff:
```python
import functools
import math

import jax
import jax.numpy as jnp
from jax import lax
from jax.experimental import pallas as pl
from jax.experimental.pallas import tpu as pltpu
from jax.sharding import PartitionSpec as P

LOG2E = math.log2(math.e)
PARTS = 4
GRAM_PARTS = 2
HOP = (7, 4)
LATE = 5
F32 = jnp.float32
BF16 = jnp.bfloat16
HIGHEST = lax.Precision.HIGHEST


def nn(a, b, precision=None):
    return lax.dot_general(a, b, (((1,), (0,)), ((), ())), precision=precision, preferred_element_type=F32)


def nt(a, b):
    return lax.dot_general(a, b, (((1,), (1,)), ((), ())), preferred_element_type=F32)


def tn(a, b):
    return lax.dot_general(a, b, (((0,), (0,)), ((), ())), preferred_element_type=F32)


def iota(shape, dim):
    return lax.broadcasted_iota(jnp.int32, shape, dim)


def column(ref, heads):
    eye = iota((heads, heads), 0) == iota((heads, heads), 1)
    spread = jnp.broadcast_to(ref[...], (heads, heads))
    return jnp.sum(jnp.where(eye, spread, 0.0), axis=1, keepdims=True)


def row_sums(values):
    high = values.astype(BF16)
    low = (values - high.astype(F32)).astype(BF16)
    both = jnp.concatenate([high, low], axis=1)
    return nt(jnp.ones((8, both.shape[1]), BF16), both)[0:1]


def pack_gram(m):
    n = m.shape[0]
    q = n // 4
    lane = iota((q, n), 1)
    second = m[q : 2 * q]
    return (
        jnp.where(lane[: q // 2] < 2 * q, second[: q // 2], pltpu.roll(second[q // 2 :], 2 * q, 1)),
        jnp.where(lane < 3 * q, m[2 * q : 3 * q], pltpu.roll(m[:q], 3 * q, 1)),
        m[3 * q :],
    )


def unpack_gram(p):
    n = p.shape[1]
    q = n // 4
    half, third = p[: q // 2], p[q // 2 : q // 2 + q]
    lower = jnp.concatenate([pltpu.roll(third, q, 1), half, pltpu.roll(half, 2 * q, 1), third, p[q // 2 + q :]], axis=0)
    return jnp.where(iota((n, n), 0) // q >= iota((n, n), 1) // q, lower, lower.T)


def kernel(
    sizes, x_ref, t_ref, b_ref, c_ref, dt_ref, alog_ref, skip_ref, bias_ref,
    gx_ref, gb_ref, gc_ref, gdt_ref, sums_ref,
    l_rows, r_rows, w_rows, g_rows, d_rows, lt_rows, s_rows, gl_rows, cq_rows, gf_rows, sk_rows,
    bt, ct, scores, cgt, decay, mixed, inner, g_cols, w_cols, gx_part, gx_out,
    contrib, srecv, snext, gram, tbuf, vbuf, pbuf, urecv, mpack, wrecv,
    gst, gb_acc, gc_acc, rb_send, rb_recv, rc_send, rc_recv, pz, px, pz_own, px_own,
    s_send, s_recv, u_send, u_recv, w_send, w_recv,
    rb_ss, rb_rs, rc_ss, rc_rs, pz_ss, pz_rs, px_ss, px_rs, gx_sem,
):
    nz, nh, ns = sizes
    heads, group, width = x_ref.shape[1:]
    state = b_ref.shape[2]
    rows = group // nh
    z = lax.axis_index("ctx")
    head_at = lax.axis_index("head")
    seq_at = lax.axis_index("seq")

    barrier = pltpu.get_barrier_semaphore()

    def greet(name, to):
        pl.semaphore_signal(barrier, inc=1, device_id={name: to}, device_id_type=pl.DeviceIdType.MESH)

    @pl.when(z > 0)
    def _():
        greet("ctx", z - 1)

    @pl.when(z < nz - 1)
    def _():
        greet("ctx", z + 1)

    for name, at, count in (("head", head_at, nh), ("seq", seq_at, ns)):
        for d in range(1, count):
            greet(name, lax.rem(at + d, count))

    rate = jnp.exp(column(alog_ref, heads))
    bias = column(bias_ref, heads)
    raw = dt_ref[0] + bias
    dt = jnp.maximum(raw, 0.0) + jnp.log1p(jnp.exp(-jnp.abs(raw)))
    upper = (iota((group, group), 0) <= iota((group, group), 1)).astype(F32)
    logs = nn(dt * (rate * -LOG2E), upper, HIGHEST)
    last = logs[:, group - 1 : group]
    rel = jnp.log(dt) * LOG2E - logs
    l_rows[...] = logs
    r_rows[...] = rel
    w_rows[...] = jnp.exp2(last + rel)
    g_rows[...] = jnp.exp2(logs)
    d_rows[...] = jnp.broadcast_to(jnp.exp2(last), (heads, width))
    lt_rows[...] = jnp.broadcast_to(last, (heads, width))
    s_rows[...] = jnp.broadcast_to(column(skip_ref, heads), (heads, width))
    bt[...] = b_ref[0].astype(F32).T
    ct[...] = c_ref[0].astype(F32).T
    scores[...] = nt(b_ref[0], c_ref[0])
    gst[...] = jnp.zeros_like(gst)
    gb_acc[...] = jnp.zeros_like(gb_acc)
    gc_acc[...] = jnp.zeros_like(gc_acc)

    met = nh + ns - 2 + jnp.where(z > 0, 1, 0) + jnp.where(z < nz - 1, 1, 0)
    pl.semaphore_wait(barrier, met)

    def chain(source, target, sends, receives, k, part, parts, step):
        piece = source.shape[1] // parts
        at = pl.ds(part * piece, piece)
        return pltpu.make_async_remote_copy(
            src_ref=source.at[k, at],
            dst_ref=target.at[k, at],
            send_sem=sends.at[k * parts + part],
            recv_sem=receives.at[k * parts + part],
            device_id={"ctx": lax.rem(z + step, nz)},
            device_id_type=pl.DeviceIdType.MESH,
        )

    def s_copy(k, part):
        return chain(snext, srecv, s_send, s_recv, k, part, PARTS, 1)

    def w_copy(k, part):
        return chain(mpack, wrecv, w_send, w_recv, k, part, GRAM_PARTS, nz - 1)

    def u_copy(k, part):
        return chain(pbuf, urecv, u_send, u_recv, k, part, PARTS, nz - 1)

    def prepare(k):
        row = pl.ds(k, 1)
        contrib[k] = nn((bt[...] * w_rows[row, :]).astype(BF16), x_ref[0, k])
        scaled_c = (ct[...] * g_rows[row, :]).astype(BF16)
        cgt[k] = scaled_c
        at = 0
        for tile in pack_gram(nt(scaled_c, scaled_c)):
            mpack[k, at : at + tile.shape[0]] = tile
            at += tile.shape[0]

    def pass_state(k):
        d = d_rows[pl.ds(k, 1), :]
        for part in range(PARTS):
            at = pl.ds(part * (state // PARTS), state // PARTS)

            @pl.when(z > 0)
            def _():
                s_copy(k, part).wait_recv()
                snext[k, at] = d * srecv[k, at] + contrib[k, at]

            @pl.when(z == 0)
            def _():
                snext[k, at] = contrib[k, at]

            @pl.when(z < nz - 1)
            def _():
                s_copy(k, part).start()

        @pl.when(z == 0)
        def _():
            srecv[k] = jnp.zeros((state, width), F32)

    def pass_gram(k):
        d = d_rows[pl.ds(k, 1), :]
        piece = mpack.shape[1] // GRAM_PARTS
        for part in range(GRAM_PARTS):
            at = pl.ds(part * piece, piece)

            @pl.when(z < nz - 1)
            def _():
                w_copy(k, part).wait_recv()
                mpack[k, at] = (d * d) * wrecv[k, at] + mpack[k, at]

            @pl.when(z > 0)
            def _():
                w_copy(k, part).start()

        @pl.when(z < nz - 1)
        def _():
            full = unpack_gram(wrecv[k])
            gram[k] = full
            tbuf[k] = nn(full, contrib[k], HIGHEST)

        @pl.when(z == nz - 1)
        def _():
            gram[k] = jnp.zeros((state, state), F32)
            urecv[k] = jnp.zeros((state, width), F32)

    def pass_adjoint(k):
        d = d_rows[pl.ds(k, 1), :]
        for part in range(PARTS):
            at = pl.ds(part * (state // PARTS), state // PARTS)

            @pl.when(z < nz - 1)
            def _():
                u_copy(k, part).wait_recv()
                pbuf[k, at] = d * (urecv[k, at] + tbuf[k, at]) + pbuf[k, at]

            @pl.when(z > 0)
            def _():
                u_copy(k, part).start()

    def local(k):
        row = pl.ds(k, 1)
        logs_row = l_rows[row, :]
        rel_col = jnp.broadcast_to(r_rows[row, :], (width, group)).T
        logs_col = jnp.broadcast_to(logs_row, (width, group)).T
        g_cols[k] = jnp.exp2(logs_col)
        w_cols[k] = jnp.exp2(rel_col + lt_rows[row, :])
        gaps = jnp.concatenate([rel_col] * (group // width), axis=1) + logs_row
        causal = iota((group, group), 1) >= iota((group, group), 0)
        scaled_decay = jnp.exp2(jnp.where(causal, gaps, -1e30))
        decay[k] = scaled_decay
        mix = (scores[...] * scaled_decay).astype(BF16)
        mixed[k] = mix
        x = x_ref[0, k]
        within = tn(mix, x)
        inner[k] = within
        error = within + s_rows[row, :] * x.astype(F32) - t_ref[0, k].astype(F32)
        pbuf[k] = nn(cgt[k], error.astype(BF16))

    def cross(k):
        vbuf[k] = nn(gram[k], snext[k], HIGHEST)

    def forward(k):
        row = pl.ds(k, 1)
        skip = s_rows[row, :]
        x = x_ref[0, k]
        wide = x.astype(F32)
        state_low = srecv[k].astype(BF16)
        growth = g_cols[k]
        output = inner[k] + nn(c_ref[0], state_low) * growth
        error = output + skip * wide - t_ref[0, k].astype(F32)
        low = error.astype(BF16)
        gst[...] += nt(x, low) * decay[k]
        grad = nn(mixed[k], low)
        gx_part[k] = grad + skip * error
        gc_acc[...] += nt((error * growth).astype(BF16), state_low)
        pulled = wide * grad
        cq_rows[row, :] = row_sums(pulled)
        gl_rows[row, :] = row_sums(low.astype(F32) * output - pulled)
        sk_rows[row, :] = jnp.sum(error * wide, axis=0, keepdims=True)

    def backward(k):
        row = pl.ds(k, 1)
        wide = x_ref[0, k].astype(F32)
        weights = w_cols[k]
        adjoint = (urecv[k] + vbuf[k]).astype(BF16)
        grad = nn(b_ref[0], adjoint) * weights
        gx_out[k] = (gx_part[k] + grad).astype(BF16)
        gx_copy(k).start()
        gb_acc[...] += nt((wide * weights).astype(BF16), adjoint)
        sums = row_sums(wide * grad)
        gl_rows[row, :] = gl_rows[row, :] - sums
        cq_rows[row, :] = cq_rows[row, :] + sums
        gf_rows[row, :] = jnp.sum(adjoint.astype(F32) * snext[k], axis=0, keepdims=True)

    def gx_copy(k):
        return pltpu.make_async_copy(gx_out.at[k], gx_ref.at[0, k], gx_sem.at[k])

    def spread(name, at, count, source_of, target, sends, receives):
        copies = []
        for d in range(1, count):
            to = lax.rem(at + d, count)
            copies.append(
                pltpu.make_async_remote_copy(
                    src_ref=source_of(to),
                    dst_ref=target.at[d],
                    send_sem=sends.at[d],
                    recv_sem=receives.at[d],
                    device_id={name: to},
                    device_id_type=pl.DeviceIdType.MESH,
                )
            )
        return copies

    def c_spread():
        return spread("head", head_at, nh, lambda to: rc_send.at[to], rc_recv, rc_ss, rc_rs)

    def send_c(k):
        gs_low = gst[...].astype(BF16)
        gb_acc[...] += nn(gs_low, c_ref[0])
        grad_c = gc_acc[...] + tn(gs_low, b_ref[0])
        for r in range(nh):
            rc_send[r] = grad_c[r * rows : (r + 1) * rows]
        for copy in c_spread():
            copy.start()

    up, down = HOP
    back = nz - 1 - z
    s_at = (z * up) // down
    w_at = (back * up) // down + jnp.minimum(back, LATE)
    u_at = w_at + heads
    l_at = jnp.where(back < 3, heads, 0)
    steps = ((nz - 1) * up) // down + LATE + 2 * heads + 1

    def step(s, carry):
        def run(work, first, count=heads):
            @pl.when(jnp.logical_and(s >= first, s < first + count))
            def _():
                work(s - first)

        run(prepare, 0)
        run(pass_state, s_at)
        run(pass_gram, w_at)
        run(local, l_at)
        run(pass_adjoint, u_at)
        run(forward, jnp.maximum(s_at, l_at))
        run(cross, jnp.maximum(s_at, w_at))
        run(send_c, jnp.maximum(s_at, l_at) + heads, 1)
        run(backward, jnp.maximum(s_at, u_at))
        return carry

    lax.fori_loop(0, steps, step, 0)

    tokens = float(group * nz * ns)
    rising = nn(gl_rows[...], (iota((group, group), 0) >= iota((group, group), 1)).astype(F32), HIGHEST)
    rising = rising + jnp.sum(gf_rows[...], axis=1, keepdims=True)
    grad_raw = (cq_rows[...] / dt - rate * rising) * (1.0 / (1.0 + jnp.exp(-raw)))
    gdt_ref[0] = grad_raw
    totals = (
        jnp.sum(rising * dt, axis=1, keepdims=True) * (-rate / tokens),
        jnp.sum(sk_rows[...], axis=1, keepdims=True) / (tokens * width),
        jnp.sum(grad_raw, axis=1, keepdims=True) / tokens,
    )
    packed = jnp.zeros((heads, width), F32)
    for q, total in enumerate(totals):
        mine = iota((heads, width), 1) == iota((heads, width), 0) + q * heads
        packed = packed + jnp.where(mine, total, 0.0)
    pz_own[0] = jnp.sum(packed, axis=0, keepdims=True)
    z_copies = spread("ctx", z, nz, lambda to: pz_own.at[0], pz, pz_ss, pz_rs)
    for copy in z_copies:
        copy.start()

    for r in range(nh):
        rb_send[r] = gb_acc[r * rows : (r + 1) * rows]
    b_copies = spread("head", head_at, nh, lambda to: rb_send.at[to], rb_recv, rb_ss, rb_rs)
    for copy in b_copies:
        copy.start()

    def drain(k, carry):
        gx_copy(k).wait()
        for part in range(PARTS):

            @pl.when(z < nz - 1)
            def _():
                s_copy(k, part).wait_send()

            @pl.when(z > 0)
            def _():
                u_copy(k, part).wait_send()

        for part in range(GRAM_PARTS):

            @pl.when(z > 0)
            def _():
                w_copy(k, part).wait_send()

        return carry

    lax.fori_loop(0, heads, drain, 0)

    c_copies = c_spread()
    whole = rc_send[head_at]
    for d, copy in enumerate(c_copies, 1):
        copy.wait_recv()
        whole = whole + rc_recv[d]
    gc_ref[0] = whole

    total = pz_own[0]
    for d, copy in enumerate(z_copies, 1):
        copy.wait_recv()
        total = total + pz[d]
    px_own[0] = total
    x_copies = spread("seq", seq_at, ns, lambda to: px_own.at[0], px, px_ss, px_rs)
    for copy in x_copies:
        copy.start()

    whole = rb_send[head_at]
    for d, copy in enumerate(b_copies, 1):
        copy.wait_recv()
        whole = whole + rb_recv[d]
    gb_ref[0] = whole

    for d, copy in enumerate(x_copies, 1):
        copy.wait_recv()
        total = total + px[d]
    sums_ref[...] = total

    for copy in z_copies + b_copies + c_copies + x_copies:
        copy.wait_send()


def deliver(gx_in, gb_in, gc_in, gdt_in, sums_in, gx, gb, gc, gdt, alog, skip, bias, hold, into, out):
    heads = gx_in.shape[1]
    arrive = [pltpu.make_async_copy(gx_in.at[0, k], hold.at[k], into.at[k]) for k in range(heads)]
    leave = [pltpu.make_async_copy(hold.at[k], gx.at[0, k], out.at[k]) for k in range(heads)]
    for copy in arrive:
        copy.start()
    gb[...] = gb_in[...]
    gc[...] = gc_in[...]
    gdt[...] = gdt_in[...]
    sums = sums_in[...]
    for q, ref in enumerate((alog, skip, bias)):
        turned = sums if q == 0 else pltpu.roll(sums, sums.shape[1] - q * heads, 1)
        ref[...] = turned[:, 0:heads]
    for k in range(heads):
        arrive[k].wait()
        leave[k].start()
    for copy in leave:
        copy.wait()


def on_device(sizes, x, t, b, c, dt, a_log, skip, bias):
    nz, nh, ns = sizes
    _, heads, group, width = x.shape
    state = b.shape[2]
    rows = group // nh
    vmem = pl.BlockSpec(memory_space=pltpu.VMEM)
    anywhere = pl.BlockSpec(memory_space=pl.ANY)
    whole = pltpu.VMEM((heads, state, width), F32)
    tall = pltpu.VMEM((heads, group, width), F32)
    line = pltpu.VMEM((heads, group), F32)
    short = pltpu.VMEM((heads, width), F32)
    flat = pltpu.VMEM((state, group), F32)
    square = pltpu.VMEM((group, group), F32)
    panel = pltpu.VMEM((group, width), F32)
    packed = pltpu.VMEM((heads, state * 5 // 8, state), F32)
    slots = pltpu.VMEM((nh, rows, width), F32)
    sems = [pltpu.SemaphoreType.DMA((heads * PARTS,))] * 4 + [pltpu.SemaphoreType.DMA((heads * GRAM_PARTS,))] * 2
    for count in (nh, nh, nz, ns):
        sems += [pltpu.SemaphoreType.DMA((count,))] * 2
    sems += [pltpu.SemaphoreType.DMA((heads,))]
    gx_shape = jax.ShapeDtypeStruct(x.shape, BF16)
    part_shape = jax.ShapeDtypeStruct((1, rows, state), F32)
    dt_shape = jax.ShapeDtypeStruct(dt.shape, F32)
    head_shape = jax.ShapeDtypeStruct((1, heads), F32)
    parts = pl.pallas_call(
        functools.partial(kernel, sizes),
        out_shape=(gx_shape, part_shape, part_shape, dt_shape, jax.ShapeDtypeStruct((1, width), F32)),
        in_specs=[vmem] * 8,
        out_specs=(anywhere,) + (vmem,) * 4,
        scratch_shapes=[line] * 4
        + [short] * 3
        + [line] * 2
        + [short] * 2
        + [
            flat,
            flat,
            square,
            pltpu.VMEM((heads, state, group), BF16),
            pltpu.VMEM((heads, group, group), F32),
            pltpu.VMEM((heads, group, group), BF16),
            tall,
            tall,
            tall,
            tall,
            pltpu.VMEM((heads, group, width), BF16),
        ]
        + [whole] * 8
        + [packed] * 2
        + [square, panel, panel]
        + [slots] * 4
        + [
            pltpu.VMEM((nz, 1, width), F32),
            pltpu.VMEM((ns, 1, width), F32),
            pltpu.VMEM((1, 1, width), F32),
            pltpu.VMEM((1, 1, width), F32),
        ]
        + sems,
        compiler_params=pltpu.CompilerParams(collective_id=0, has_side_effects=True),
        name="mixer",
    )(x, t, b, c, dt, a_log.reshape(1, heads), skip.reshape(1, heads), bias.reshape(1, heads))
    outs = pl.pallas_call(
        deliver,
        out_shape=(gx_shape, part_shape, part_shape, dt_shape) + (head_shape,) * 3,
        in_specs=[anywhere] + [vmem] * 4,
        out_specs=(anywhere,) + (vmem,) * 6,
        scratch_shapes=[pltpu.VMEM((heads, group, width), BF16)] + [pltpu.SemaphoreType.DMA((heads,))] * 2,
        name="deliver",
    )(*parts)
    return outs[:4] + tuple(o.reshape(heads) for o in outs[4:])


def solution(mesh):
    sizes = tuple(mesh.shape[name] for name in ("ctx", "head", "seq"))
    return jax.shard_map(
        functools.partial(on_device, sizes),
        mesh=mesh,
        in_specs=(
            P("seq", "head", "ctx", None),
            P("seq", "head", "ctx", None),
            P("seq", "ctx", None),
            P("seq", "ctx", None),
            P("seq", "head", "ctx"),
            P("head"),
            P("head"),
            P("head"),
        ),
        out_specs=(
            P("seq", "head", "ctx", None),
            P("seq", ("ctx", "head"), None),
            P("seq", ("ctx", "head"), None),
            P("seq", "head", "ctx"),
            P("head"),
            P("head"),
            P("head"),
        ),
        check_vma=False,
    )
```

time: 113 us -> 101 us (0.89)
  Pallas kernels: 107 us -> 100 us
  local copies, waits for them, and re-layouts: 5.69 us -> 0 us
    pallas_call x1 -> x2, Pallas kernels: 107 us -> 100 us  [the longest x1 96.8 us: on_device(): pl.pallas_call(functools.partial(kernel, sizes), out_shape=(gx_shape, par...]
    unnamed x19 -> x0, local copies, waits for them, and re-layouts: 5.69 us -> none
where the time goes in v2:
time: 101 us
  Pallas kernels  100 us (99%)
    pallas_call x1, Pallas kernels, on_device(): pl.pallas_call(functools.partial(kernel, sizes), out_shape=(gx_shape, par...  96.8 us
    pallas_call x1, Pallas kernels, on_device(): pl.pallas_call(deliver, out_shape=(gx_shape, part_shape, part_shape, dt_s...  3.19 us

profile of v2, /device:TPU:1, one launch (start us, length us, event | category | flops | bytes accessed | tf_op | source)
XLA Modules:
  0.0 100.7 jit_solution(1028919577733424194)
XLA Ops:
  0.6 96.8 %mixer.1 = (bf16[1,8,256,128]{3,2,1,0:T(8,128)(2,1)}, f32[1,32,128]{2,1,0:T(8,128)}, f32[1,32,128]{2,1,0:T(8,128)}, f32[1,8,256]{2,1,0:T(8,128)}, f32[1,128]{1,0:T(1,128)}) custom-call(bf16[1,8,256,128]{3,2,1,0:T(8,128)(2,1)} %x_ref.1, bf16[1,8,256,128]{3,2,1,0:T(8,128)(2,1)} %t_ref.1, bf16[1,256,128]{2,1,0:T(8,128)(2,1)} %b_ref.1, ...), custom_call_target="tpu_custom_call" | custom-call | tf_op jit(solution)/shard_map/mixer/pallas_call | solution.py:458
  97.5 3.2 %deliver.1 = (bf16[1,8,256,128]{3,2,1,0:T(8,128)(2,1)}, f32[1,32,128]{2,1,0:T(8,128)}, f32[1,32,128]{2,1,0:T(8,128)}, f32[1,8,256]{2,1,0:T(8,128)}, f32[1,8]{1,0...) custom-call(bf16[1,8,256,128]{3,2,1,0:T(8,128)(2,1)} %get-tuple-element.19.gx_in, f32[1,32,128]{2,1,0:T(8,128)} %get-tuple-element.20.gb_in, ...), custom_call_target="tpu_custom_call" | custom-call | tf_op jit(solution)/shard_map/deliver/pallas_call | solution.py:494

commit v3 on v2

--- a/solution.py
+++ b/solution.py
@@ -11,8 +11,9 @@
 LOG2E = math.log2(math.e)
 PARTS = 4
 GRAM_PARTS = 2
-HOP = (7, 4)
-LATE = 5
+HOP = 8
+LATE = 10
+SOON, NEAR, FAR = 3, 7, 12
 F32 = jnp.float32
 BF16 = jnp.bfloat16
 HIGHEST = lax.Precision.HIGHEST
@@ -67,15 +68,37 @@
     return jnp.where(iota((n, n), 0) // q >= iota((n, n), 1) // q, lower, lower.T)
 
 
+def plan(z, nz, heads, where, most):
+    back = nz - 1 - z
+    span = heads * PARTS
+    grams = heads * GRAM_PARTS
+    soon, near, far = z < nz * SOON // 16, z < nz * NEAR // 16, z >= nz * FAR // 16
+    s_at = z * HOP
+    w_at = back * HOP + where(back > 0, LATE, 0)
+    u_at = w_at + grams + grams // 4
+    both = most(s_at, u_at)
+    l_at = where(soon, s_at + span, where(far, u_at - PARTS, 2 * heads))
+    l_by = where(far, PARTS, 2)
+    f_at = most(where(soon, l_at, where(near, s_at, both) + PARTS - 1), l_at)
+    f_by = where(soon, 2, PARTS)
+    inside = most(w_at + GRAM_PARTS - 1, s_at + span // 2 + 1)
+    c_at = where(near, inside, where(far, both + PARTS - 1, both + span))
+    c_by = where(near, GRAM_PARTS, where(far, PARTS, 2))
+    b_at = most(where(near, both + PARTS - 1, where(far, both + PARTS - 1, both + span)), most(c_at, f_at))
+    b_by = where(near, PARTS, where(far, PARTS, 2))
+    return s_at, w_at, u_at, l_at, l_by, f_at, f_by, c_at, c_by, b_at, b_by, b_at + heads * PARTS + 2
+
+
 def kernel(
-    sizes, x_ref, t_ref, b_ref, c_ref, dt_ref, alog_ref, skip_ref, bias_ref,
-    gx_ref, gb_ref, gc_ref, gdt_ref, sums_ref,
+    sizes, x_in, t_in, b_in, c_in, dt_in, alog_in, skip_in, bias_in,
+    gx_ref, gb_out, gc_out, gdt_out, sums_out,
+    x_ref, t_ref, b_ref, c_ref, dt_ref, alog_ref, skip_ref, bias_ref, gb_ref, gc_ref, gdt_ref, sums_ref,
     l_rows, r_rows, w_rows, g_rows, d_rows, lt_rows, s_rows, gl_rows, cq_rows, gf_rows, sk_rows,
     bt, ct, scores, cgt, decay, mixed, inner, g_cols, w_cols, gx_part, gx_out,
     contrib, srecv, snext, gram, tbuf, vbuf, pbuf, urecv, mpack, wrecv,
     gst, gb_acc, gc_acc, rb_send, rb_recv, rc_send, rc_recv, pz, px, pz_own, px_own,
     s_send, s_recv, u_send, u_recv, w_send, w_recv,
-    rb_ss, rb_rs, rc_ss, rc_rs, pz_ss, pz_rs, px_ss, px_rs, gx_sem,
+    rb_ss, rb_rs, rc_ss, rc_rs, pz_ss, pz_rs, px_ss, px_rs, gx_sem, in_sem, out_sem,
 ):
     nz, nh, ns = sizes
     heads, group, width = x_ref.shape[1:]
@@ -101,6 +124,16 @@
     for name, at, count in (("head", head_at, nh), ("seq", seq_at, ns)):
         for d in range(1, count):
             greet(name, lax.rem(at + d, count))
+
+    pairs = (
+        (dt_in, dt_ref), (alog_in, alog_ref), (bias_in, bias_ref), (skip_in, skip_ref),
+        (b_in, b_ref), (c_in, c_ref), (x_in, x_ref), (t_in, t_ref),
+    )
+    arriving = [pltpu.make_async_copy(source, target, in_sem.at[i]) for i, (source, target) in enumerate(pairs)]
+    for copy in arriving:
+        copy.start()
+    for copy in arriving[:6]:
+        copy.wait()
 
     rate = jnp.exp(column(alog_ref, heads))
     bias = column(bias_ref, heads)
@@ -124,12 +157,14 @@
     gb_acc[...] = jnp.zeros_like(gb_acc)
     gc_acc[...] = jnp.zeros_like(gc_acc)
 
+    for copy in arriving[6:]:
+        copy.wait()
     met = nh + ns - 2 + jnp.where(z > 0, 1, 0) + jnp.where(z < nz - 1, 1, 0)
     pl.semaphore_wait(barrier, met)
 
     def chain(source, target, sends, receives, k, part, parts, step):
         piece = source.shape[1] // parts
-        at = pl.ds(part * piece, piece)
+        at = pl.ds(pl.multiple_of(part * piece, piece), piece)
         return pltpu.make_async_remote_copy(
             src_ref=source.at[k, at],
             dst_ref=target.at[k, at],
@@ -158,43 +193,43 @@
             mpack[k, at : at + tile.shape[0]] = tile
             at += tile.shape[0]
 
-    def pass_state(k):
+    def pass_state(p):
+        k = p // PARTS
+        part = lax.rem(p, PARTS)
         d = d_rows[pl.ds(k, 1), :]
-        for part in range(PARTS):
-            at = pl.ds(part * (state // PARTS), state // PARTS)
-
-            @pl.when(z > 0)
-            def _():
-                s_copy(k, part).wait_recv()
-                snext[k, at] = d * srecv[k, at] + contrib[k, at]
-
-            @pl.when(z == 0)
-            def _():
-                snext[k, at] = contrib[k, at]
-
-            @pl.when(z < nz - 1)
-            def _():
-                s_copy(k, part).start()
+        at = pl.ds(pl.multiple_of(part * (state // PARTS), state // PARTS), state // PARTS)
+
+        @pl.when(z > 0)
+        def _():
+            s_copy(k, part).wait_recv()
+            snext[k, at] = d * srecv[k, at] + contrib[k, at]
 
         @pl.when(z == 0)
         def _():
-            srecv[k] = jnp.zeros((state, width), F32)
-
-    def pass_gram(k):
+            snext[k, at] = contrib[k, at]
+            srecv[k, at] = jnp.zeros((state // PARTS, width), F32)
+
+        @pl.when(z < nz - 1)
+        def _():
+            s_copy(k, part).start()
+
+    def pass_gram(q):
+        k = q // GRAM_PARTS
+        part = lax.rem(q, GRAM_PARTS)
         d = d_rows[pl.ds(k, 1), :]
         piece = mpack.shape[1] // GRAM_PARTS
-        for part in range(GRAM_PARTS):
-            at = pl.ds(part * piece, piece)
-
-            @pl.when(z < nz - 1)
-            def _():
-                w_copy(k, part).wait_recv()
-                mpack[k, at] = (d * d) * wrecv[k, at] + mpack[k, at]
-
-            @pl.when(z > 0)
-            def _():
-                w_copy(k, part).start()
-
+        at = pl.ds(pl.multiple_of(part * piece, piece), piece)
+
+        @pl.when(z < nz - 1)
+        def _():
+            w_copy(k, part).wait_recv()
+            mpack[k, at] = (d * d) * wrecv[k, at] + mpack[k, at]
+
+        @pl.when(z > 0)
+        def _():
+            w_copy(k, part).start()
+
+    def widen(k):
         @pl.when(z < nz - 1)
         def _():
             full = unpack_gram(wrecv[k])
@@ -206,19 +241,20 @@
             gram[k] = jnp.zeros((state, state), F32)
             urecv[k] = jnp.zeros((state, width), F32)
 
-    def pass_adjoint(k):
+    def pass_adjoint(p):
+        k = p // PARTS
+        part = lax.rem(p, PARTS)
         d = d_rows[pl.ds(k, 1), :]
-        for part in range(PARTS):
-            at = pl.ds(part * (state // PARTS), state // PARTS)
-
-            @pl.when(z < nz - 1)
-            def _():
-                u_copy(k, part).wait_recv()
-                pbuf[k, at] = d * (urecv[k, at] + tbuf[k, at]) + pbuf[k, at]
-
-            @pl.when(z > 0)
-            def _():
-                u_copy(k, part).start()
+        at = pl.ds(pl.multiple_of(part * (state // PARTS), state // PARTS), state // PARTS)
+
+        @pl.when(z < nz - 1)
+        def _():
+            u_copy(k, part).wait_recv()
+            pbuf[k, at] = d * (urecv[k, at] + tbuf[k, at]) + pbuf[k, at]
+
+        @pl.when(z > 0)
+        def _():
+            u_copy(k, part).start()
 
     def local(k):
         row = pl.ds(k, 1)
@@ -306,29 +342,34 @@
         for copy in c_spread():
             copy.start()
 
-    up, down = HOP
-    back = nz - 1 - z
-    s_at = (z * up) // down
-    w_at = (back * up) // down + jnp.minimum(back, LATE)
-    u_at = w_at + heads
-    l_at = jnp.where(back < 3, heads, 0)
-    steps = ((nz - 1) * up) // down + LATE + 2 * heads + 1
+    s_at, w_at, u_at, l_at, l_by, f_at, f_by, c_at, c_by, b_at, b_by, _ = plan(z, nz, heads, jnp.where, jnp.maximum)
+    span = heads * PARTS
+    grams = heads * GRAM_PARTS
+    steps = max(plan(at, nz, heads, lambda c, x, y: x if c else y, max)[-1] for at in range(nz))
 
     def step(s, carry):
-        def run(work, first, count=heads):
+        def relay(work, first, count):
             @pl.when(jnp.logical_and(s >= first, s < first + count))
             def _():
                 work(s - first)
 
-        run(prepare, 0)
-        run(pass_state, s_at)
-        run(pass_gram, w_at)
-        run(local, l_at)
-        run(pass_adjoint, u_at)
-        run(forward, jnp.maximum(s_at, l_at))
-        run(cross, jnp.maximum(s_at, w_at))
-        run(send_c, jnp.maximum(s_at, l_at) + heads, 1)
-        run(backward, jnp.maximum(s_at, u_at))
+        def run(work, first, by, count=heads):
+            past = s - first
+
+            @pl.when(jnp.logical_and(past >= 0, jnp.logical_and(past < by * count, lax.rem(past, by) == 0)))
+            def _():
+                work(past // by)
+
+        run(prepare, 0, 2)
+        relay(pass_gram, w_at, grams)
+        run(widen, w_at + GRAM_PARTS - 1, GRAM_PARTS)
+        run(local, l_at, l_by)
+        relay(pass_adjoint, u_at, span)
+        relay(pass_state, s_at, span)
+        run(forward, f_at, f_by)
+        run(cross, c_at, c_by)
+        run(backward, b_at, b_by)
+        run(send_c, f_at + f_by * heads, 1, 1)
         return carry
 
     lax.fori_loop(0, steps, step, 0)
@@ -338,6 +379,8 @@
     rising = rising + jnp.sum(gf_rows[...], axis=1, keepdims=True)
     grad_raw = (cq_rows[...] / dt - rate * rising) * (1.0 / (1.0 + jnp.exp(-raw)))
     gdt_ref[0] = grad_raw
+    gdt_copy = pltpu.make_async_copy(gdt_ref, gdt_out, out_sem.at[0])
+    gdt_copy.start()
     totals = (
         jnp.sum(rising * dt, axis=1, keepdims=True) * (-rate / tokens),
         jnp.sum(sk_rows[...], axis=1, keepdims=True) / (tokens * width),
@@ -386,6 +429,8 @@
         copy.wait_recv()
         whole = whole + rc_recv[d]
     gc_ref[0] = whole
+    gc_copy = pltpu.make_async_copy(gc_ref, gc_out, out_sem.at[1])
+    gc_copy.start()
 
     total = pz_own[0]
     for d, copy in enumerate(z_copies, 1):
@@ -401,32 +446,41 @@
         copy.wait_recv()
         whole = whole + rb_recv[d]
     gb_ref[0] = whole
+    gb_copy = pltpu.make_async_copy(gb_ref, gb_out, out_sem.at[2])
+    gb_copy.start()
 
     for d, copy in enumerate(x_copies, 1):
         copy.wait_recv()
         total = total + px[d]
     sums_ref[...] = total
+    sums_copy = pltpu.make_async_copy(sums_ref, sums_out, out_sem.at[3])
+    sums_copy.start()
 
     for copy in z_copies + b_copies + c_copies + x_copies:
         copy.wait_send()
-
-
-def deliver(gx_in, gb_in, gc_in, gdt_in, sums_in, gx, gb, gc, gdt, alog, skip, bias, hold, into, out):
-    heads = gx_in.shape[1]
-    arrive = [pltpu.make_async_copy(gx_in.at[0, k], hold.at[k], into.at[k]) for k in range(heads)]
-    leave = [pltpu.make_async_copy(hold.at[k], gx.at[0, k], out.at[k]) for k in range(heads)]
+    for copy in (gdt_copy, gc_copy, gb_copy, sums_copy):
+        copy.wait()
+
+
+def deliver(*refs):
+    ins, outs, (gx, gb, gc, gdt, sums_ref, *heads_refs), (into, out) = refs[:5], refs[5:12], refs[12:20], refs[20:]
+    heads = gx.shape[1]
+    held = (gx, gb, gc, gdt)
+    arrive = [pltpu.make_async_copy(ins[4], sums_ref, into.at[4])]
+    arrive += [pltpu.make_async_copy(a, b, into.at[i]) for i, (a, b) in enumerate(zip(ins[:4], held))]
     for copy in arrive:
         copy.start()
-    gb[...] = gb_in[...]
-    gc[...] = gc_in[...]
-    gdt[...] = gdt_in[...]
-    sums = sums_in[...]
-    for q, ref in enumerate((alog, skip, bias)):
+    arrive[0].wait()
+    sums = sums_ref[...]
+    for q, ref in enumerate(heads_refs):
         turned = sums if q == 0 else pltpu.roll(sums, sums.shape[1] - q * heads, 1)
         ref[...] = turned[:, 0:heads]
-    for k in range(heads):
-        arrive[k].wait()
-        leave[k].start()
+    leave = [pltpu.make_async_copy(a, b, out.at[i]) for i, (a, b) in enumerate(zip(held + tuple(heads_refs), outs))]
+    for copy in leave[4:]:
+        copy.start()
+    for i in range(4):
+        arrive[i + 1].wait()
+        leave[i].start()
     for copy in leave:
         copy.wait()
 
@@ -436,7 +490,6 @@
     _, heads, group, width = x.shape
     state = b.shape[2]
     rows = group // nh
-    vmem = pl.BlockSpec(memory_space=pltpu.VMEM)
     anywhere = pl.BlockSpec(memory_space=pl.ANY)
     whole = pltpu.VMEM((heads, state, width), F32)
     tall = pltpu.VMEM((heads, group, width), F32)
@@ -450,7 +503,7 @@
     sems = [pltpu.SemaphoreType.DMA((heads * PARTS,))] * 4 + [pltpu.SemaphoreType.DMA((heads * GRAM_PARTS,))] * 2
     for count in (nh, nh, nz, ns):
         sems += [pltpu.SemaphoreType.DMA((count,))] * 2
-    sems += [pltpu.SemaphoreType.DMA((heads,))]
+    sems += [pltpu.SemaphoreType.DMA((count,)) for count in (heads, 8, 4)]
     gx_shape = jax.ShapeDtypeStruct(x.shape, BF16)
     part_shape = jax.ShapeDtypeStruct((1, rows, state), F32)
     dt_shape = jax.ShapeDtypeStruct(dt.shape, F32)
@@ -458,9 +511,13 @@
     parts = pl.pallas_call(
         functools.partial(kernel, sizes),
         out_shape=(gx_shape, part_shape, part_shape, dt_shape, jax.ShapeDtypeStruct((1, width), F32)),
-        in_specs=[vmem] * 8,
-        out_specs=(anywhere,) + (vmem,) * 4,
-        scratch_shapes=[line] * 4
+        in_specs=[anywhere] * 8,
+        out_specs=(anywhere,) * 5,
+        scratch_shapes=[pltpu.VMEM(a.shape, a.dtype) for a in (x, t, b, c, dt)]
+        + [pltpu.VMEM((1, heads), F32)] * 3
+        + [pltpu.VMEM((1, rows, state), F32)] * 2
+        + [pltpu.VMEM(dt.shape, F32), pltpu.VMEM((1, width), F32)]
+        + [line] * 4
         + [short] * 3
         + [line] * 2
         + [short] * 2
@@ -494,9 +551,11 @@
     outs = pl.pallas_call(
         deliver,
         out_shape=(gx_shape, part_shape, part_shape, dt_shape) + (head_shape,) * 3,
-        in_specs=[anywhere] + [vmem] * 4,
-        out_specs=(anywhere,) + (vmem,) * 6,
-        scratch_shapes=[pltpu.VMEM((heads, group, width), BF16)] + [pltpu.SemaphoreType.DMA((heads,))] * 2,
+        in_specs=[anywhere] * 5,
+        out_specs=(anywhere,) * 7,
+        scratch_shapes=[pltpu.VMEM(a.shape, a.dtype) for a in parts]
+        + [pltpu.VMEM((1, heads), F32)] * 3
+        + [pltpu.SemaphoreType.DMA((5,)), pltpu.SemaphoreType.DMA((7,))],
         name="deliver",
     )(*parts)
     return outs[:4] + tuple(o.reshape(heads) for o in outs[4:])

time: 101 us -> 89.7 us (0.89)
  Pallas kernels: 100 us -> 88.9 us
    pallas_call x1, Pallas kernels: 96.8 us -> 87 us  [on_device(): pl.pallas_call(functools.partial(kernel, sizes), out_shape=(gx_shape, par...]
    pallas_call x1, Pallas kernels: 3.19 us -> 1.96 us  [on_device(): pl.pallas_call(deliver, out_shape=(gx_shape, part_shape, part_shape, dt_s...]
where the time goes in v3:
time: 89.7 us; the launch traced here: 89.6 us
  Pallas kernels  88.9 us (99%)
    pallas_call x1, Pallas kernels, on_device(): pl.pallas_call(functools.partial(kernel, sizes), out_shape=(gx_shape, par...  87 us
    pallas_call x1, Pallas kernels, on_device(): pl.pallas_call(deliver, out_shape=(gx_shape, part_shape, part_shape, dt_s...  1.96 us

profile of v3, /device:TPU:1, one launch (start us, length us, event | category | flops | bytes accessed | tf_op | source)
XLA Modules:
  0.0 89.6 jit_solution(386386800312306723)
XLA Ops:
  0.6 87.0 %mixer.1 = (bf16[1,8,256,128]{3,2,1,0:T(8,128)(2,1)}, f32[1,32,128]{2,1,0:T(8,128)}, f32[1,32,128]{2,1,0:T(8,128)}, f32[1,8,256]{2,1,0:T(8,128)}, f32[1,128]{1,0:T(1,128)}) custom-call(bf16[1,8,256,128]{3,2,1,0:T(8,128)(2,1)} %x_in.1, bf16[1,8,256,128]{3,2,1,0:T(8,128)(2,1)} %t_in.1, bf16[1,256,128]{2,1,0:T(8,128)(2,1)} %b_in.1, bf16[1,256,128]{2,1,0:T(8,128)(2,1)} %c_in.1, ...), custom_call_target="tpu_custom_call" | custom-call | tf_op jit(solution)/shard_map/mixer/pallas_call | solution.py:511
  87.6 2.0 %deliver.1 = (bf16[1,8,256,128]{3,2,1,0:T(8,128)(2,1)}, f32[1,32,128]{2,1,0:T(8,128)}, f32[1,32,128]{2,1,0:T(8,128)}, f32[1,8,256]{2,1,0:T(8,128)}, f32[1,8]{1,0...) custom-call(bf16[1,8,256,128]{3,2,1,0:T(8,128)(2,1)} %get-tuple-element.19.refs_0_, f32[1,32,128]{2,1,0:T(8,128)} %get-tuple-element.20.refs_1_, ...), custom_call_target="tpu_custom_call" | custom-call | tf_op jit(solution)/shard_map/deliver/pallas_call | solution.py:551

commit v4 on v3

--- a/solution.py
+++ b/solution.py
@@ -11,8 +11,9 @@
 LOG2E = math.log2(math.e)
 PARTS = 4
 GRAM_PARTS = 2
-HOP = 8
-LATE = 10
+SLOTS = 2
+HOP = 9
+LATE = 5
 SOON, NEAR, FAR = 3, 7, 12
 F32 = jnp.float32
 BF16 = jnp.bfloat16
@@ -70,23 +71,22 @@
 
 def plan(z, nz, heads, where, most):
     back = nz - 1 - z
-    span = heads * PARTS
-    grams = heads * GRAM_PARTS
+    span = heads * SLOTS
     soon, near, far = z < nz * SOON // 16, z < nz * NEAR // 16, z >= nz * FAR // 16
-    s_at = z * HOP
-    w_at = back * HOP + where(back > 0, LATE, 0)
-    u_at = w_at + grams + grams // 4
+    s_at = z * HOP // 2
+    w_at = back * HOP // 2 + where(back > 0, LATE, 0)
+    u_at = w_at + heads + heads // 4
     both = most(s_at, u_at)
-    l_at = where(soon, s_at + span, where(far, u_at - PARTS, 2 * heads))
-    l_by = where(far, PARTS, 2)
-    f_at = most(where(soon, l_at, where(near, s_at, both) + PARTS - 1), l_at)
-    f_by = where(soon, 2, PARTS)
-    inside = most(w_at + GRAM_PARTS - 1, s_at + span // 2 + 1)
-    c_at = where(near, inside, where(far, both + PARTS - 1, both + span))
-    c_by = where(near, GRAM_PARTS, where(far, PARTS, 2))
-    b_at = most(where(near, both + PARTS - 1, where(far, both + PARTS - 1, both + span)), most(c_at, f_at))
-    b_by = where(near, PARTS, where(far, PARTS, 2))
-    return s_at, w_at, u_at, l_at, l_by, f_at, f_by, c_at, c_by, b_at, b_by, b_at + heads * PARTS + 2
+    l_at = where(soon, s_at + span, where(far, u_at - SLOTS, heads))
+    l_by = where(far, SLOTS, 1)
+    f_at = most(where(soon, l_at, where(near, s_at, both) + SLOTS - 1), l_at)
+    f_by = where(soon, 1, SLOTS)
+    inside = most(w_at, s_at + span)
+    c_at = where(near, inside, where(far, both + SLOTS - 1, both + span))
+    c_by = where(far, SLOTS, 1)
+    b_at = most(where(near, both + SLOTS - 1, where(far, both + SLOTS - 1, both + span)), most(c_at, f_at))
+    b_by = where(near, SLOTS, where(far, SLOTS, 1))
+    return s_at, w_at, u_at, l_at, l_by, f_at, f_by, c_at, c_by, b_at, b_by, b_at + b_by * (heads - 1) + 1, f_at + f_by * heads + 1
 
 
 def kernel(
@@ -159,6 +159,18 @@
 
     for copy in arriving[6:]:
         copy.wait()
+    def prepare(k):
+        row = pl.ds(k, 1)
+        scaled_c = (ct[...] * g_rows[row, :]).astype(BF16)
+        cgt[k] = scaled_c
+        at = 0
+        for tile in pack_gram(nt(scaled_c, scaled_c)):
+            mpack[k, at : at + tile.shape[0]] = tile
+            at += tile.shape[0]
+        contrib[k] = nn((bt[...] * w_rows[row, :]).astype(BF16), x_ref[0, k])
+
+    prepare(0)
+
     met = nh + ns - 2 + jnp.where(z > 0, 1, 0) + jnp.where(z < nz - 1, 1, 0)
     pl.semaphore_wait(barrier, met)
 
@@ -183,51 +195,41 @@
     def u_copy(k, part):
         return chain(pbuf, urecv, u_send, u_recv, k, part, PARTS, nz - 1)
 
-    def prepare(k):
-        row = pl.ds(k, 1)
-        contrib[k] = nn((bt[...] * w_rows[row, :]).astype(BF16), x_ref[0, k])
-        scaled_c = (ct[...] * g_rows[row, :]).astype(BF16)
-        cgt[k] = scaled_c
-        at = 0
-        for tile in pack_gram(nt(scaled_c, scaled_c)):
-            mpack[k, at : at + tile.shape[0]] = tile
-            at += tile.shape[0]
-
     def pass_state(p):
-        k = p // PARTS
-        part = lax.rem(p, PARTS)
+        k = p // SLOTS
         d = d_rows[pl.ds(k, 1), :]
-        at = pl.ds(pl.multiple_of(part * (state // PARTS), state // PARTS), state // PARTS)
-
-        @pl.when(z > 0)
-        def _():
-            s_copy(k, part).wait_recv()
-            snext[k, at] = d * srecv[k, at] + contrib[k, at]
-
-        @pl.when(z == 0)
-        def _():
-            snext[k, at] = contrib[k, at]
-            srecv[k, at] = jnp.zeros((state // PARTS, width), F32)
-
-        @pl.when(z < nz - 1)
-        def _():
-            s_copy(k, part).start()
-
-    def pass_gram(q):
-        k = q // GRAM_PARTS
-        part = lax.rem(q, GRAM_PARTS)
+        for sub in range(PARTS // SLOTS):
+            part = lax.rem(p, SLOTS) * (PARTS // SLOTS) + sub
+            at = pl.ds(pl.multiple_of(part * (state // PARTS), state // PARTS), state // PARTS)
+
+            @pl.when(z > 0)
+            def _():
+                s_copy(k, part).wait_recv()
+                snext[k, at] = d * srecv[k, at] + contrib[k, at]
+
+            @pl.when(z == 0)
+            def _():
+                snext[k, at] = contrib[k, at]
+                srecv[k, at] = jnp.zeros((state // PARTS, width), F32)
+
+            @pl.when(z < nz - 1)
+            def _():
+                s_copy(k, part).start()
+
+    def pass_gram(k):
         d = d_rows[pl.ds(k, 1), :]
         piece = mpack.shape[1] // GRAM_PARTS
-        at = pl.ds(pl.multiple_of(part * piece, piece), piece)
-
-        @pl.when(z < nz - 1)
-        def _():
-            w_copy(k, part).wait_recv()
-            mpack[k, at] = (d * d) * wrecv[k, at] + mpack[k, at]
-
-        @pl.when(z > 0)
-        def _():
-            w_copy(k, part).start()
+        for part in range(GRAM_PARTS):
+            at = pl.ds(part * piece, piece)
+
+            @pl.when(z < nz - 1)
+            def _():
+                w_copy(k, part).wait_recv()
+                mpack[k, at] = (d * d) * wrecv[k, at] + mpack[k, at]
+
+            @pl.when(z > 0)
+            def _():
+                w_copy(k, part).start()
 
     def widen(k):
         @pl.when(z < nz - 1)
@@ -242,19 +244,24 @@
             urecv[k] = jnp.zeros((state, width), F32)
 
     def pass_adjoint(p):
-        k = p // PARTS
-        part = lax.rem(p, PARTS)
+        k = p // SLOTS
         d = d_rows[pl.ds(k, 1), :]
-        at = pl.ds(pl.multiple_of(part * (state // PARTS), state // PARTS), state // PARTS)
-
-        @pl.when(z < nz - 1)
-        def _():
-            u_copy(k, part).wait_recv()
-            pbuf[k, at] = d * (urecv[k, at] + tbuf[k, at]) + pbuf[k, at]
-
-        @pl.when(z > 0)
-        def _():
-            u_copy(k, part).start()
+        for sub in range(PARTS // SLOTS):
+            part = lax.rem(p, SLOTS) * (PARTS // SLOTS) + sub
+            at = pl.ds(pl.multiple_of(part * (state // PARTS), state // PARTS), state // PARTS)
+
+            @pl.when(z == 0)
+            def _():
+                u_copy(k, part).wait_recv()
+
+            @pl.when(jnp.logical_and(z > 0, z < nz - 1))
+            def _():
+                u_copy(k, part).wait_recv()
+                pbuf[k, at] = d * (urecv[k, at] + tbuf[k, at]) + pbuf[k, at]
+
+            @pl.when(z > 0)
+            def _():
+                u_copy(k, part).start()
 
     def local(k):
         row = pl.ds(k, 1)
@@ -316,7 +323,7 @@
 
     def spread(name, at, count, source_of, target, sends, receives):
         copies = []
-        for d in range(1, count):
+        for d in sorted(range(1, count), key=lambda d: abs(2 * d - count)):
             to = lax.rem(at + d, count)
             copies.append(
                 pltpu.make_async_remote_copy(
@@ -342,10 +349,9 @@
         for copy in c_spread():
             copy.start()
 
-    s_at, w_at, u_at, l_at, l_by, f_at, f_by, c_at, c_by, b_at, b_by, _ = plan(z, nz, heads, jnp.where, jnp.maximum)
-    span = heads * PARTS
-    grams = heads * GRAM_PARTS
-    steps = max(plan(at, nz, heads, lambda c, x, y: x if c else y, max)[-1] for at in range(nz))
+    s_at, w_at, u_at, l_at, l_by, f_at, f_by, c_at, c_by, b_at, b_by, *_ = plan(z, nz, heads, jnp.where, jnp.maximum)
+    span = heads * SLOTS
+    steps = max(max(plan(at, nz, heads, lambda c, x, y: x if c else y, max)[-2:]) for at in range(nz))
 
     def step(s, carry):
         def relay(work, first, count):
@@ -353,16 +359,19 @@
             def _():
                 work(s - first)
 
+        def times(by):
+            return SLOTS // by if isinstance(by, int) else jnp.where(by == SLOTS, 1, SLOTS)
+
         def run(work, first, by, count=heads):
-            past = s - first
-
-            @pl.when(jnp.logical_and(past >= 0, jnp.logical_and(past < by * count, lax.rem(past, by) == 0)))
-            def _():
-                work(past // by)
-
-        run(prepare, 0, 2)
-        relay(pass_gram, w_at, grams)
-        run(widen, w_at + GRAM_PARTS - 1, GRAM_PARTS)
+            past = (s - first) * times(by)
+
+            @pl.when(jnp.logical_and(past >= 0, jnp.logical_and(past < SLOTS * count, lax.rem(past, SLOTS) == 0)))
+            def _():
+                work(past // SLOTS)
+
+        relay(lambda k: prepare(k + 1), 0, heads - 1)
+        relay(pass_gram, w_at, heads)
+        relay(widen, w_at, heads)
         run(local, l_at, l_by)
         relay(pass_adjoint, u_at, span)
         relay(pass_state, s_at, span)
@@ -373,6 +382,12 @@
         return carry
 
     lax.fori_loop(0, steps, step, 0)
+
+    for r in range(nh):
+        rb_send[r] = gb_acc[r * rows : (r + 1) * rows]
+    b_copies = spread("head", head_at, nh, lambda to: rb_send.at[to], rb_recv, rb_ss, rb_rs)
+    for copy in b_copies:
+        copy.start()
 
     tokens = float(group * nz * ns)
     rising = nn(gl_rows[...], (iota((group, group), 0) >= iota((group, group), 1)).astype(F32), HIGHEST)
@@ -395,12 +410,6 @@
     for copy in z_copies:
         copy.start()
 
-    for r in range(nh):
-        rb_send[r] = gb_acc[r * rows : (r + 1) * rows]
-    b_copies = spread("head", head_at, nh, lambda to: rb_send.at[to], rb_recv, rb_ss, rb_rs)
-    for copy in b_copies:
-        copy.start()
-
     def drain(k, carry):
         gx_copy(k).wait()
         for part in range(PARTS):
@@ -425,16 +434,18 @@
 
     c_copies = c_spread()
     whole = rc_send[head_at]
-    for d, copy in enumerate(c_copies, 1):
+    for copy in c_copies:
         copy.wait_recv()
+    for d in range(1, nh):
         whole = whole + rc_recv[d]
     gc_ref[0] = whole
     gc_copy = pltpu.make_async_copy(gc_ref, gc_out, out_sem.at[1])
     gc_copy.start()
 
     total = pz_own[0]
-    for d, copy in enumerate(z_copies, 1):
+    for copy in z_copies:
         copy.wait_recv()
+    for d in range(1, nz):
         total = total + pz[d]
     px_own[0] = total
     x_copies = spread("seq", seq_at, ns, lambda to: px_own.at[0], px, px_ss, px_rs)
@@ -442,15 +453,17 @@
         copy.start()
 
     whole = rb_send[head_at]
-    for d, copy in enumerate(b_copies, 1):
+    for copy in b_copies:
         copy.wait_recv()
+    for d in range(1, nh):
         whole = whole + rb_recv[d]
     gb_ref[0] = whole
     gb_copy = pltpu.make_async_copy(gb_ref, gb_out, out_sem.at[2])
     gb_copy.start()
 
-    for d, copy in enumerate(x_copies, 1):
+    for copy in x_copies:
         copy.wait_recv()
+    for d in range(1, ns):
         total = total + px[d]
     sums_ref[...] = total
     sums_copy = pltpu.make_async_copy(sums_ref, sums_out, out_sem.at[3])

time: 89.7 us -> 88.1 us (0.982)
  Pallas kernels: 88.9 us -> 87 us
    pallas_call x1, Pallas kernels: 87 us -> 85.1 us  [on_device(): pl.pallas_call(functools.partial(kernel, sizes), out_shape=(gx_shape, par...]
where the time goes in v4:
time: 88.1 us; the launch traced here: 87.7 us
  Pallas kernels  87 us (99%)
    pallas_call x1, Pallas kernels, on_device(): pl.pallas_call(functools.partial(kernel, sizes), out_shape=(gx_shape, par...  85.1 us
    pallas_call x1, Pallas kernels, on_device(): pl.pallas_call(deliver, out_shape=(gx_shape, part_shape, part_shape, dt_s...  1.96 us

profile of v4, /device:TPU:1, one launch (start us, length us, event | category | flops | bytes accessed | tf_op | source)
XLA Modules:
  0.0 87.7 jit_solution(3786230983437451004)
XLA Ops:
  0.6 85.1 %mixer.1 = (bf16[1,8,256,128]{3,2,1,0:T(8,128)(2,1)}, f32[1,32,128]{2,1,0:T(8,128)}, f32[1,32,128]{2,1,0:T(8,128)}, f32[1,8,256]{2,1,0:T(8,128)}, f32[1,128]{1,0:T(1,128)}) custom-call(bf16[1,8,256,128]{3,2,1,0:T(8,128)(2,1)} %x_in.1, bf16[1,8,256,128]{3,2,1,0:T(8,128)(2,1)} %t_in.1, bf16[1,256,128]{2,1,0:T(8,128)(2,1)} %b_in.1, bf16[1,256,128]{2,1,0:T(8,128)(2,1)} %c_in.1, ...), custom_call_target="tpu_custom_call" | custom-call | tf_op jit(solution)/shard_map/mixer/pallas_call | solution.py:524
  85.7 2.0 %deliver.1 = (bf16[1,8,256,128]{3,2,1,0:T(8,128)(2,1)}, f32[1,32,128]{2,1,0:T(8,128)}, f32[1,32,128]{2,1,0:T(8,128)}, f32[1,8,256]{2,1,0:T(8,128)}, f32[1,8]{1,0...) custom-call(bf16[1,8,256,128]{3,2,1,0:T(8,128)(2,1)} %get-tuple-element.19.refs_0_, f32[1,32,128]{2,1,0:T(8,128)} %get-tuple-element.20.refs_1_, ...), custom_call_target="tpu_custom_call" | custom-call | tf_op jit(solution)/shard_map/deliver/pallas_call | solution.py:564
